TPU v7x, 32 devices: a whole 2x2x4 slice. The times are simulated.
32 devices in a mesh: dp: 16 (over z, y, x), tensor: 2 (over core).
Axes of the slice: x: 2, y: 2, z: 4, core: 2. Of those that a mesh axis runs over, the one named last changes fastest.
Arguments:
- tokens: bfloat16 [32768, 768], P('dp'), may hold values from -6 to 6
- first_values: bfloat16 [32768, 384], P('dp'), may hold values from -6 to 6
- seq_count: int32 [16], P('dp'), may hold values from 1 to 2, as said below
- skip_map: int32 [6], P('tensor'), may hold values from 0 to 5, as said below
- norm1_gain: float32 [768], replicated, may hold values from 0.5 to 1.5
- norm1_shift: float32 [768], replicated, may hold values from -1 to 1
- query_weight: bfloat16 [768, 768], P(None, 'tensor'), may hold values from -0.3125 to 0.3125
- key_weight: bfloat16 [768, 768], P(None, 'tensor'), may hold values from -0.3125 to 0.3125
- value_weight: bfloat16 [768, 384], P(None, 'tensor'), may hold values from -0.21875 to 0.21875
- out_weight: bfloat16 [768, 768], P('tensor'), may hold values from -1.75 to 1.75
- norm2_gain: float32 [768], replicated, may hold values from 0.5 to 1.5
- norm2_shift: float32 [768], replicated, may hold values from -1 to 1
- up_weight: bfloat16 [768, 3072], P(None, 'tensor'), may hold values from -0.21875 to 0.21875
- down_weight: bfloat16 [3072, 768], P('tensor'), may hold values from -0.109375 to 0.109375
- cotangent: bfloat16 [32768, 768], P('dp'), may hold values from -6 to 6
Outputs:
- layer_out: float32 [32768, 768], P('dp')
- input_grad: float32 [32768, 768], P('dp')
- first_value_grad: float32 [32768, 384], P('dp', 'tensor')
- norm1_gain_grad: float32 [768], P('dp')
- norm1_shift_grad: float32 [768], P('dp')
- query_weight_grad: float32 [768, 768], P('dp', 'tensor')
- key_weight_grad: float32 [768, 768], P('dp', 'tensor')
- value_weight_grad: float32 [768, 384], P('dp', 'tensor')
- out_weight_grad: float32 [768, 768], P('tensor', 'dp')
- norm2_gain_grad: float32 [768], P('dp')
- norm2_shift_grad: float32 [768], P('dp')
- up_weight_grad: float32 [768, 3072], P('dp', 'tensor')
- down_weight_grad: float32 [3072, 768], P('tensor', 'dp')
Inputs may be any that keep to these rules, and one draw needn't show every extreme that they name: `seq_count`: some index of dp holds 2 live sequences in every draw; slots below the count are live. `skip_map`: A permutation: each first-layer value head is read by exactly one slot; the slots of each index of tensor read exactly one head of the other index's half.
All inputs are finite; a program needn't handle non-finite values.
Results may differ from a plain program's by a relative error of at most 0.012.
The roundings to bfloat16 on the way count: a program that leaves them out, or rounds other values in their place, can miss the bound.
Values sent between devices are 32-bit elements; how exact they have to be, the bound alone decides.
A program may use at most 192 MiB of HBM per device.

v0:
```python
import jax
import jax.numpy as jnp
from jax import lax
from jax.sharding import PartitionSpec as P

HEAD_DIM = 64
SEQ_LEN = 1024
SKIP_HEADS = 6


eps_norm = 1e-05
neg_fill = -1e30
precise = lax.Precision.HIGHEST


def normalize(values_in, norm_gain, norm_shift):
    average = jnp.mean(values_in, axis=-1, keepdims=True)
    centered = values_in - average
    variance = jnp.mean(centered * centered, axis=-1, keepdims=True)
    return centered * lax.rsqrt(variance + eps_norm) * norm_gain + norm_shift


def smooth_gate(upper):
    return jax.nn.gelu(upper, approximate=True)


def causal_scores(query_block, seq_keys, first_row):
    block_rows = query_block.shape[0]
    length = seq_keys.shape[0]
    score_scale = query_block.shape[2] ** (-0.5)
    scores = (
        jnp.einsum("qhd,khd->hqk", query_block, seq_keys, preferred_element_type=jnp.float32)
        * score_scale
    )
    query_pos = first_row + lax.iota(jnp.int32, block_rows)
    key_pos = lax.iota(jnp.int32, length)
    return jnp.where(key_pos[None, None, :] <= query_pos[None, :, None], scores, neg_fill)


def attend_forward(queries, keys_low, values):

    def one_sequence(packed):
        seq_query, seq_keys, seq_values = packed
        length = seq_query.shape[0]
        block_rows = min(512, length)
        count_blocks = length // block_rows
        query_blocks = seq_query.reshape((count_blocks, block_rows) + seq_query.shape[1:])
        block_starts = lax.iota(jnp.int32, count_blocks) * block_rows

        def one_block(block_pair):
            query_block, first_row = block_pair
            masked = causal_scores(query_block, seq_keys, first_row)
            row_peak = jnp.max(masked, axis=-1)
            expo_terms = jnp.exp(masked - row_peak[..., None])
            row_total = jnp.sum(expo_terms, axis=-1)
            weights_low = (expo_terms / row_total[..., None]).astype(jnp.bfloat16)
            mixed_rows = jnp.einsum(
                "hqk,khd->qhd", weights_low, seq_values, preferred_element_type=jnp.float32
            )
            return (mixed_rows.astype(jnp.bfloat16), row_peak, row_total)

        attended, peaks_all, totals_all = lax.map(one_block, (query_blocks, block_starts))
        return (attended.reshape(seq_query.shape), peaks_all, totals_all)

    return lax.map(one_sequence, (queries, keys_low, values))


def attend_backward(queries, keys_low, values, grad_heads, peaks_all, totals_all):

    def one_sequence(packed):
        seq_query, seq_keys, seq_values, seq_grad, seq_peaks, seq_totals = packed
        length, head_count, head_width = seq_query.shape
        block_rows = min(512, length)
        count_blocks = length // block_rows
        block_shape = (count_blocks, block_rows, head_count, head_width)
        score_scale = head_width ** (-0.5)
        block_starts = lax.iota(jnp.int32, count_blocks) * block_rows

        def one_block(carry, block_pack):
            key_acc, value_acc = carry
            query_block, grad_block, row_peak, row_total, first_row = block_pack
            masked = causal_scores(query_block, seq_keys, first_row)
            soft_full = jnp.exp(masked - row_peak[..., None]) / row_total[..., None]
            weights_low = soft_full.astype(jnp.bfloat16)
            value_acc = value_acc + jnp.einsum(
                "hqk,qhd->khd", weights_low, grad_block, preferred_element_type=jnp.float32
            )
            grad_weights = jnp.einsum(
                "qhd,khd->hqk", grad_block, seq_values, preferred_element_type=jnp.float32
            )
            row_dot = jnp.sum(soft_full * grad_weights, axis=-1, keepdims=True)
            score_grad = (soft_full * (grad_weights - row_dot)).astype(jnp.bfloat16)
            query_grad = (
                jnp.einsum("hqk,khd->qhd", score_grad, seq_keys, preferred_element_type=jnp.float32)
                * score_scale
            )
            key_acc = (
                key_acc
                + jnp.einsum(
                    "hqk,qhd->khd", score_grad, query_block, preferred_element_type=jnp.float32
                )
                * score_scale
            )
            return ((key_acc, value_acc), query_grad.astype(jnp.bfloat16))

        zeros_acc = jnp.zeros((length, head_count, head_width), jnp.float32)
        (key_acc, value_acc), query_grads = lax.scan(
            one_block,
            (zeros_acc, zeros_acc),
            (
                seq_query.reshape(block_shape),
                seq_grad.reshape(block_shape),
                seq_peaks,
                seq_totals,
                block_starts,
            ),
        )
        return (query_grads.reshape(seq_query.shape), key_acc.astype(jnp.bfloat16), value_acc)

    return lax.map(one_sequence, (queries, keys_low, values, grad_heads, peaks_all, totals_all))


def on_device(
    tokens,
    first_values,
    seq_count,
    skip_map,
    norm1_gain,
    norm1_shift,
    query_weight,
    key_weight,
    value_weight,
    out_weight,
    norm2_gain,
    norm2_shift,
    up_weight,
    down_weight,
    cotangent,
):
    rows_dev = tokens.shape[0]
    head_count = query_weight.shape[1] // HEAD_DIM
    fresh_count = value_weight.shape[1] // HEAD_DIM
    seq_shape = (rows_dev // SEQ_LEN, SEQ_LEN, head_count, HEAD_DIM)
    inputs = tokens.astype(jnp.float32)
    normed_one, pull_one = jax.vjp(normalize, inputs, norm1_gain, norm1_shift)
    normed_low = normed_one.astype(jnp.bfloat16)
    queries = jnp.dot(normed_low, query_weight, preferred_element_type=jnp.float32).astype(
        jnp.bfloat16
    )
    keys_low = jnp.dot(normed_low, key_weight, preferred_element_type=jnp.float32).astype(
        jnp.bfloat16
    )
    fresh_values = jnp.dot(normed_low, value_weight, preferred_element_type=jnp.float32).astype(
        jnp.bfloat16
    )
    slot_select = skip_map[:, None] == lax.iota(jnp.int32, SKIP_HEADS)[None, :]
    picked = jnp.einsum(
        "tjd,ij->tid",
        first_values.reshape(rows_dev, SKIP_HEADS, HEAD_DIM),
        slot_select.astype(jnp.bfloat16),
        preferred_element_type=jnp.float32,
    ).astype(jnp.bfloat16)
    values = jnp.concatenate(
        [fresh_values.reshape(rows_dev, fresh_count, HEAD_DIM), picked], axis=1
    )
    query_seq = queries.reshape(seq_shape)
    key_seq = keys_low.reshape(seq_shape)
    value_seq = values.reshape(seq_shape)
    attended, peaks_all, totals_all = attend_forward(query_seq, key_seq, value_seq)
    attended_low = attended.reshape(rows_dev, head_count * HEAD_DIM)
    attn_part = jnp.dot(attended_low, out_weight, preferred_element_type=jnp.float32)
    mixed = inputs + lax.psum(attn_part, "tensor")
    normed_two, pull_two = jax.vjp(normalize, mixed, norm2_gain, norm2_shift)
    normed_two_low = normed_two.astype(jnp.bfloat16)
    upper = jnp.dot(normed_two_low, up_weight, preferred_element_type=jnp.float32)
    activ, gate_pull = jax.vjp(smooth_gate, upper)
    activ_low = activ.astype(jnp.bfloat16)
    down_part = jnp.dot(activ_low, down_weight, preferred_element_type=jnp.float32)
    layer_out = mixed + lax.psum(down_part, "tensor")
    slot_rows = lax.iota(jnp.int32, rows_dev) // SEQ_LEN
    live_rows = (slot_rows < seq_count[0]).astype(jnp.float32)
    grad_out = cotangent.astype(jnp.float32) * live_rows[:, None]
    grad_low = grad_out.astype(jnp.bfloat16)
    down_grad = jnp.einsum("rf,rd->fd", activ_low, grad_low, preferred_element_type=jnp.float32)
    grad_activ = jnp.dot(grad_low, down_weight.T, preferred_element_type=jnp.float32)
    grad_upper = gate_pull(grad_activ)[0].astype(jnp.bfloat16)
    up_grad = jnp.einsum(
        "rd,rf->df", normed_two_low, grad_upper, preferred_element_type=jnp.float32
    )
    two_part = jnp.dot(grad_upper, up_weight.T, preferred_element_type=jnp.float32)
    grad_two = lax.psum(two_part, "tensor")
    grad_mixed_norm, gain2_grad, shift2_grad = pull_two(grad_two)
    grad_mixed = grad_out + grad_mixed_norm
    grad_attn_low = grad_mixed.astype(jnp.bfloat16)
    out_grad = jnp.einsum(
        "rh,rd->hd", attended_low, grad_attn_low, preferred_element_type=jnp.float32
    )
    grad_heads = jnp.dot(grad_attn_low, out_weight.T, preferred_element_type=jnp.float32).astype(
        jnp.bfloat16
    )
    query_grads, key_grads, value_grads = attend_backward(
        query_seq, key_seq, value_seq, grad_heads.reshape(seq_shape), peaks_all, totals_all
    )
    query_low = query_grads.reshape(rows_dev, head_count * HEAD_DIM)
    key_low = key_grads.reshape(rows_dev, head_count * HEAD_DIM)
    value_rows = value_grads.reshape(rows_dev, head_count, HEAD_DIM)
    fresh_low = (
        value_rows[:, :fresh_count].astype(jnp.bfloat16).reshape(rows_dev, fresh_count * HEAD_DIM)
    )
    skip_rows = value_rows[:, fresh_count:]
    first_part = jnp.einsum(
        "tid,ij->tjd", skip_rows, slot_select.astype(jnp.float32), precision=precise
    ).reshape(rows_dev, SKIP_HEADS * HEAD_DIM)
    query_grad = jnp.einsum("rd,rh->dh", normed_low, query_low, preferred_element_type=jnp.float32)
    key_grad = jnp.einsum("rd,rh->dh", normed_low, key_low, preferred_element_type=jnp.float32)
    value_grad = jnp.einsum("rd,rh->dh", normed_low, fresh_low, preferred_element_type=jnp.float32)
    one_part = (
        jnp.dot(query_low, query_weight.T, preferred_element_type=jnp.float32)
        + jnp.dot(key_low, key_weight.T, preferred_element_type=jnp.float32)
        + jnp.dot(fresh_low, value_weight.T, preferred_element_type=jnp.float32)
    )
    grad_one = lax.psum(one_part, "tensor")
    first_grad = lax.psum_scatter(first_part, "tensor", scatter_dimension=1, tiled=True)
    grad_in_norm, gain1_grad, shift1_grad = pull_one(grad_one)
    input_grad = grad_mixed + grad_in_norm
    (
        gain1_total,
        shift1_total,
        query_total,
        key_total,
        value_total,
        out_total,
        gain2_total,
        shift2_total,
        up_total,
        down_total,
    ) = (
        lax.psum_scatter(gain1_grad, "dp", scatter_dimension=0, tiled=True),
        lax.psum_scatter(shift1_grad, "dp", scatter_dimension=0, tiled=True),
        lax.psum_scatter(query_grad, "dp", scatter_dimension=0, tiled=True),
        lax.psum_scatter(key_grad, "dp", scatter_dimension=0, tiled=True),
        lax.psum_scatter(value_grad, "dp", scatter_dimension=0, tiled=True),
        lax.psum_scatter(out_grad, "dp", scatter_dimension=1, tiled=True),
        lax.psum_scatter(gain2_grad, "dp", scatter_dimension=0, tiled=True),
        lax.psum_scatter(shift2_grad, "dp", scatter_dimension=0, tiled=True),
        lax.psum_scatter(up_grad, "dp", scatter_dimension=0, tiled=True),
        lax.psum_scatter(down_grad, "dp", scatter_dimension=1, tiled=True),
    )
    return (
        layer_out,
        input_grad,
        first_grad,
        gain1_total,
        shift1_total,
        query_total,
        key_total,
        value_total,
        out_total,
        gain2_total,
        shift2_total,
        up_total,
        down_total,
    )


def solution(mesh):
    placed = (
        P("dp", None),
        P("dp", None),
        P("dp"),
        P("tensor"),
        P(),
        P(),
        P(None, "tensor"),
        P(None, "tensor"),
        P(None, "tensor"),
        P("tensor", None),
        P(),
        P(),
        P(None, "tensor"),
        P("tensor", None),
        P("dp", None),
    )
    return jax.shard_map(
        on_device,
        mesh=mesh,
        in_specs=placed,
        out_specs=(
            P("dp", None),
            P("dp", None),
            P("dp", "tensor"),
            P("dp"),
            P("dp"),
            P("dp", "tensor"),
            P("dp", "tensor"),
            P("dp", "tensor"),
            P("tensor", "dp"),
            P("dp"),
            P("dp"),
            P("dp", "tensor"),
            P("tensor", "dp"),
        ),
        check_vma=False,
    )
```

profile of v0, /device:TPU:0, one launch (start us, length us, event | category | flops | bytes accessed | tf_op | source)
XLA Modules:
  0.0 1368.7 jit_solution(5389367105774942727)
XLA Ops:
  65.4 86.7 %while.58 = (s32[]{:T(128)}, bf16[2,1024,6,64]{3,2,1,0:T(8,128)(2,1)}, f32[2,2,6,512]{3,2,1,0:T(8,128)}, f32[2,2,6,512]{3,2,1,0:T(8,128)S(1)}, bf16[2,1024,6,64]...) while((s32[]{:T(128)}, ...), condition=%wide.region_7.8_spmd, body=%wide.region_2.7_spmd.sunk | while | flops 843770368 | bytes 65536428 | solution.py:65
  73.5 28.0 %while.61 = (s32[]{:T(128)}, bf16[2,512,6,64]{1,3,2,0:T(8,128)(2,1)}, f32[2,6,512]{2,1,0:T(8,128)S(1)}, f32[2,6,512]{2,1,0:T(8,128)S(1)}, s32[2]{0:T(128)S(1)}, ...) while((s32[]{:T(128)}, ...), condition=%wide.region_6.6_spmd, body=%wide.region_3.5_spmd.sunk | while | flops 843770368 | bytes 51781844 | solution.py:62
  116.9 28.0 %while.61 = (s32[]{:T(128)}, bf16[2,512,6,64]{1,3,2,0:T(8,128)(2,1)}, f32[2,6,512]{2,1,0:T(8,128)S(1)}, f32[2,6,512]{2,1,0:T(8,128)S(1)}, s32[2]{0:T(128)S(1)}, ...) while((s32[]{:T(128)}, ...), condition=%wide.region_6.6_spmd, body=%wide.region_3.5_spmd.sunk | while | flops 843770368 | bytes 51781844 | solution.py:62
  152.1 6.1 reshape.230
  158.2 6.0 fusion.77
  165.2 33.9 %all-reduce.10.cloned.1.call-done = f32[2048,768]{1,0:T(8,128)} async-done(((f32[2048,768]{1,0:T(8,128)}), f32[2048,768]{1,0:T(8,128)}) %all-reduce.10.cloned.1.call-update) | async-done | bytes 6291472 | tf_op jit(solution)/shard_map/psum | solution.py:172
  206.3 8.3 fusion.72
  214.5 13.7 %fusion.38 = bf16[2048,1536]{1,0:T(8,128)(2,1)S(1)} fusion(f32[2048,1536]{1,0:T(8,128)} %fusion.72, bf16[1536,768]{1,0:T(8,128)(2,1)S(1)} %copy-done.65, bf16[2048,768]{1,0:T(8,128)(2,1)S(1)} %copy-done.19, f32[2048]{0:T(1024)S(1)} %fusion.62), kind=kOutput, calls=%fused_computation.71 | convolution fusion | flops 4899471360 | bytes 24387584 | tf_op jit(solution)/shard_map/dot_general | solution.py:185
  230.9 6.9 fusion.78
  239.5 12.0 fusion.73
  251.5 19.8 %all-reduce.12.cloned.1.call-done = f32[2048,768]{1,0:T(8,128)} async-done(((f32[2048,768]{1,0:T(8,128)}), f32[2048,768]{1,0:T(8,128)}) %all-reduce.12.cloned.1.call-update) | async-done | bytes 6291472 | tf_op jit(solution)/shard_map/psum | solution.py:191
  271.3 6.4 multiply_reduce_fusion.1
  294.4 185.1 %while.60 = (s32[]{:T(128)}, bf16[2,1024,6,64]{3,2,1,0:T(8,128)(2,1)}, bf16[2,1024,6,64]{1,3,2,0:T(8,128)(2,1)}, f32[2,1024,6,64]{1,0,3,2:T(2,128)}, bf16[2,1024...) while((s32[]{:T(128)}, ...), condition=%wide.region_19.20_spmd, body=%wide.region_15.19_spmd.sunk | while | flops 2047997440 | bytes 193598400 | solution.py:120
  302.7 45.7 %while.62 = (s32[]{:T(128)}, f32[1024,6,64]{0,2,1:T(8,128)}, f32[1024,6,64]{0,2,1:T(8,128)}, bf16[2,512,6,64]{1,3,2,0:T(8,128)(2,1)}, bf16[2,512,6,64]{1,3,2,0:T...) while((s32[]{:T(128)}, f32[1024,6,64]{0,2,1:T(8,128)}, ...), condition=%wide.region_18.18_spmd.clone, body=%wide.region_16.17_spmd.clone.sunk | while | flops 2047604224 | bytes 159814224 | solution.py:107
  356.0 27.5 %dynamic_update_slice.59 = f32[2,1024,6,64]{1,0,3,2:T(2,128)} dynamic-update-slice(f32[2,1024,6,64]{1,0,3,2:T(2,128)} %get-tuple-element.862, f32[1,1024,6,64]{1,0,3,2:T(1,128)S(1)} %copy.123, s32[]{:T(128)S(6)} %copy.176, s32[]{:T(128)} %constant.118.clone.1..sunk.1, s32[]{:T(128)} %constant.118.clone.1..sunk.1, s32[]{:T(128)} %constant.118.clone.1..sunk.1) | dynamic-update-slice | bytes 3145732 | tf_op jit(solution)/shard_map/while/body/jit(dynamic_update_index_in_dim)/dynamic_update_slice | solution.py:120
  395.0 45.7 %while.62 = (s32[]{:T(128)}, f32[1024,6,64]{0,2,1:T(8,128)}, f32[1024,6,64]{0,2,1:T(8,128)}, bf16[2,512,6,64]{1,3,2,0:T(8,128)(2,1)}, bf16[2,512,6,64]{1,3,2,0:T...) while((s32[]{:T(128)}, f32[1024,6,64]{0,2,1:T(8,128)}, ...), condition=%wide.region_18.18_spmd.clone, body=%wide.region_16.17_spmd.clone.sunk | while | flops 2047604224 | bytes 159814224 | solution.py:107
  399.7 6.0 multiply_reduce_fusion.5
  421.7 6.0 multiply_reduce_fusion.5
  448.3 27.5 %dynamic_update_slice.59 = f32[2,1024,6,64]{1,0,3,2:T(2,128)} dynamic-update-slice(f32[2,1024,6,64]{1,0,3,2:T(2,128)} %get-tuple-element.862, f32[1,1024,6,64]{1,0,3,2:T(1,128)S(1)} %copy.123, s32[]{:T(128)S(6)} %copy.176, s32[]{:T(128)} %constant.118.clone.1..sunk.1, s32[]{:T(128)} %constant.118.clone.1..sunk.1, s32[]{:T(128)} %constant.118.clone.1..sunk.1) | dynamic-update-slice | bytes 3145732 | tf_op jit(solution)/shard_map/while/body/jit(dynamic_update_index_in_dim)/dynamic_update_slice | solution.py:120
  515.6 6.5 fusion.82
  522.2 11.5 fusion.55
  533.9 14.3 %fusion.71 = f32[768,1536]{1,0:T(8,128)} fusion(bf16[2048,1536]{1,0:T(8,128)(2,1)} %copy-done.72, f32[2048,768]{1,0:T(8,128)} %copy-done.8, f32[768]{0:T(1024)S(1)} %copy-done.68, f32[768]{0:T(1024)S(1)} %copy-done.61, f32[2048]{0:T(1024)S(1)} %copy-done.55, f32[2048]{0:T(1024)S(1)} %copy-done.47), kind=kOutput, calls=%fused_computation.135 | convolution fusion | flops 4839702528 | bytes 17324032 | tf_op jit(solution)/shard_map/rd,rf->df/dot_general | solution.py:187
  557.9 8.6 add.143
  572.1 77.1 %all-reduce.4 = (f32[768]{0:T(1024)S(1)}, f32[768]{0:T(1024)S(1)}, f32[768]{0:T(1024)S(1)}, f32[768]{0:T(1024)S(1)}) all-reduce(f32[768]{0:T(1024)S(1)} %get-tuple-element.342, f32[768]{0:T(1024)S(1)} %get-tuple-element.345, f32[768]{0:T(1024)S(1)} %copy-done.58, ...), channel_id=3, replica_groups=mesh['dp'=16,'tensor'=2] {'dp'}, use_global_device_ids=true, to_apply=%region_25.26.clone | all-reduce | flops 3072 | bytes 24576
  651.5 11.0 add_add_fusion.2
  662.5 17.6 %reduce-scatter.14.cloned.1.call-done = f32[48,192]{1,0:T(8,128)} async-done(((f32[768,192]{1,0:T(8,128)}), f32[48,192]{1,0:T(8,128)}) %reduce-scatter.14.cloned.1.call-update) | async-done | bytes 36880 | tf_op jit(solution)/shard_map/reduce_scatter | solution.py:242
  680.1 127.8 %reduce-scatter.16.cloned.1.call-done = f32[384,48]{0,1:T(8,128)} async-done(((f32[384,768]{0,1:T(8,128)}), f32[384,48]{0,1:T(8,128)}) %reduce-scatter.16.cloned.1.call-update) | async-done | bytes 73744 | tf_op jit(solution)/shard_map/reduce_scatter | solution.py:243
  807.9 127.8 %reduce-scatter.10.cloned.1.call-done = f32[48,384]{1,0:T(8,128)} async-done(((f32[768,384]{1,0:T(8,128)}), f32[48,384]{1,0:T(8,128)}) %reduce-scatter.10.cloned.1.call-update) | async-done | bytes 73744 | tf_op jit(solution)/shard_map/reduce_scatter | solution.py:240
  935.7 128.0 %reduce-scatter.12.cloned.1.call-done = f32[48,384]{1,0:T(8,128)} async-done(((f32[768,384]{1,0:T(8,128)}), f32[48,384]{1,0:T(8,128)}) %reduce-scatter.12.cloned.1.call-update) | async-done | bytes 73744 | tf_op jit(solution)/shard_map/reduce_scatter | solution.py:241
  1063.7 142.1 %reduce-scatter.20.cloned.1.call-done = f32[1536,48]{0,1:T(8,128)} async-done(((f32[1536,768]{0,1:T(8,128)}), f32[1536,48]{0,1:T(8,128)}) %reduce-scatter.20.cloned.1.call-update) | async-done | bytes 294928 | tf_op jit(solution)/shard_map/reduce_scatter | solution.py:247
  1205.8 143.1 %reduce-scatter.18.cloned.1.call-done = f32[48,1536]{1,0:T(8,128)} async-done(((f32[768,1536]{1,0:T(8,128)}), f32[48,1536]{1,0:T(8,128)}) %reduce-scatter.18.cloned.1.call-update) | async-done | bytes 294928 | tf_op jit(solution)/shard_map/reduce_scatter | solution.py:246
  1349.0 12.6 reduce-scatter.8.cloned.1.call-done
  (446 shorter events, 342.4 us)
Async XLA Ops:
  7.2 199.1 %copy-start = (bf16[768,1536]{1,0:T(8,128)(2,1)S(1)}, bf16[768,1536]{1,0:T(8,128)(2,1)}, u32[]{:S(2)}) copy-start(bf16[768,1536]{1,0:T(8,128)(2,1)} %param.35) | copy-start | bytes 7077892
  7.2 191.9 %all-reduce.10.cloned.1.call-start = ((), (), s32[]{:S(2)}) async-start(), calls=%async_computation.7 | async-start | bytes 12582912 | tf_op jit(solution)/shard_map/psum | solution.py:172
  9.8 10.0 copy-start.56
  9.8 10.0 copy-start.62
  9.8 12.8 copy-start.42
  12.8 9.8 copy-start.44
  19.8 9.9 copy-start.30
  38.9 9.5 copy-start.34
  164.3 107.0 %all-reduce.12.cloned.1.call-start = ((), (), s32[]{:S(2)}) async-start(), calls=%async_computation.8 | async-start | bytes 12582912 | tf_op jit(solution)/shard_map/psum | solution.py:191
  165.2 117.0 %copy-start.48 = (f32[2048]{0:T(1024)}, f32[2048]{0:T(1024)S(1)}, u32[]{:S(2)}) copy-start(f32[2048]{0:T(1024)S(1)} %fusion.62) | copy-start | bytes 24580
  203.6 74.2 %copy-start.46 = (f32[2048]{0:T(1024)}, f32[2048]{0:T(1024)S(1)}, u32[]{:S(2)}) copy-start(f32[2048]{0:T(1024)S(1)} %broadcast_multiply_fusion) | copy-start | bytes 24580
  206.2 71.5 %copy-start.54 = (f32[2048]{0:T(1024)}, f32[2048]{0:T(1024)S(1)}, u32[]{:S(2)}) copy-start(f32[2048]{0:T(1024)S(1)} %fusion.64) | copy-start | bytes 24580
  237.9 319.9 %all-reduce.14.cloned.1.call-start = ((), (), s32[]{:S(2)}) async-start(), calls=%async_computation.16 | async-start | bytes 25165824 | tf_op jit(solution)/shard_map/psum | solution.py:179
  351.9 34.9 %copy-start.39 = (f32[2,2,6,512]{3,2,1,0:T(8,128)S(1)}, f32[2,2,6,512]{3,2,1,0:T(8,128)}, u32[]{:S(2)}) copy-start(f32[2,2,6,512]{3,2,1,0:T(8,128)} %copy-done.38) | copy-start | bytes 147460 | tf_op jit(solution)/shard_map/while
  444.2 34.9 %copy-start.39 = (f32[2,2,6,512]{3,2,1,0:T(8,128)S(1)}, f32[2,2,6,512]{3,2,1,0:T(8,128)}, u32[]{:S(2)}) copy-start(f32[2,2,6,512]{3,2,1,0:T(8,128)} %copy-done.38) | copy-start | bytes 147460 | tf_op jit(solution)/shard_map/while
  500.7 179.4 %reduce-scatter.14.cloned.1.call-start = ((), (), s32[]{:S(2)}) async-start(), calls=%async_computation.12 | async-start | bytes 835584 | tf_op jit(solution)/shard_map/reduce_scatter | solution.py:242
  504.9 303.0 %reduce-scatter.16.cloned.1.call-start = ((), (), s32[]{:S(2)}) async-start(), calls=%async_computation.13 | async-start | bytes 1253376 | tf_op jit(solution)/shard_map/reduce_scatter | solution.py:243
  509.7 426.0 %reduce-scatter.10.cloned.1.call-start = ((), (), s32[]{:S(2)}) async-start(), calls=%async_computation.10 | async-start | bytes 1253376 | tf_op jit(solution)/shard_map/reduce_scatter | solution.py:240
  515.5 548.2 %reduce-scatter.12.cloned.1.call-start = ((), (), s32[]{:S(2)}) async-start(), calls=%async_computation.11 | async-start | bytes 1253376 | tf_op jit(solution)/shard_map/reduce_scatter | solution.py:241
  522.1 11.7 copy-start.47
  522.1 11.7 copy-start.55
  522.2 11.7 copy-start.61
  522.2 11.7 copy-start.68
  522.2 683.7 %reduce-scatter.20.cloned.1.call-start = ((), (), s32[]{:S(2)}) async-start(), calls=%async_computation.15 | async-start | bytes 5013504 | tf_op jit(solution)/shard_map/reduce_scatter | solution.py:247
  533.8 815.2 %reduce-scatter.18.cloned.1.call-start = ((), (), s32[]{:S(2)}) async-start(), calls=%async_computation.14 | async-start | bytes 5013504 | tf_op jit(solution)/shard_map/reduce_scatter | solution.py:246
  548.2 813.4 %reduce-scatter.8.cloned.1.call-start = ((), (), s32[]{:S(2)}) async-start(), calls=%async_computation.9 | async-start | bytes 4718592 | tf_op jit(solution)/shard_map/reduce_scatter | solution.py:223
  557.8 8.6 copy-start.9
  557.8 9.1 copy-start.11
  557.8 9.1 copy-start.43
  557.9 9.1 copy-start.57
  568.9 82.6 %copy-start.51 = (f32[2048]{0:T(1024)S(1)}, f32[2048]{0:T(1024)}, u32[]{:S(2)}) copy-start(f32[2048]{0:T(1024)} %copy-done.50) | copy-start | bytes 24580
  651.5 710.1 %copy-start.1 = (bf16[768,1536]{1,0:T(8,128)(2,1)S(1)}, bf16[768,1536]{1,0:T(8,128)(2,1)}, u32[]{:S(2)}) copy-start(bf16[768,1536]{1,0:T(8,128)(2,1)} %param.35) | copy-start | bytes 7077892
  (100 other events, 335.5 us)
Sparse Core Ops, SparseCore 0:
  164.4 34.7 all-reduce.9
  238.0 33.2 all-reduce.11
  500.8 50.6 all-reduce.13
  556.6 123.3 reduce-scatter.13
  685.2 122.6 reduce-scatter.15
  813.1 122.5 reduce-scatter.9
  941.0 122.6 reduce-scatter.11
  1069.4 136.3 reduce-scatter.19
  1212.4 136.5 reduce-scatter.17
  1351.6 9.9 reduce-scatter.7
where the time goes:
time: 1380 us; the launch traced here: 1370 us
  waiting for transfers between devices  753 us (55%)
  matrix products  213 us (15%)
  local copies, waits for them, and re-layouts  209 us (15%)
  other arithmetic  96.2 us (7%)
  blocking collectives  77.1 us (6%)
  between operations  16.5 us (1%)
    reduce_scatter x1, waiting for transfers between devices, on_device(): lax.psum_scatter(up_grad, 'dp', scatter_dimension=0, tiled=True)  143 us
    reduce_scatter x1, waiting for transfers between devices, on_device(): lax.psum_scatter(down_grad, 'dp', scatter_dimension=1, tiled=True)  142 us
    reduce_scatter x1, waiting for transfers between devices, on_device(): lax.psum_scatter(key_grad, 'dp', scatter_dimension=0, tiled=True)  128 us
    reduce_scatter x1, waiting for transfers between devices, on_device(): lax.psum_scatter(out_grad, 'dp', scatter_dimension=1, tiled=True)  128 us
    reduce_scatter x1, waiting for transfers between devices, on_device(): lax.psum_scatter(query_grad, 'dp', scatter_dimension=0, tiled=True)  128 us
    unnamed x1, blocking collectives  77.1 us
    dynamic_update_slice x4, local copies, waits for them, and re-layouts, attend_backward(): lax.map(one_sequence, (queries, keys_low, values, grad_heads, peaks_all,...  58.2 us
    dot_general x8, matrix products, causal_scores(): jnp.einsum('qhd,khd->hqk', query_block, seq_keys, preferred_element_type=...  37.4 us
  transfers between devices with their start and end apart: 10, of which 9 were waited for; matrix products, arithmetic and copies ran while one was open for 7% of the time, Pallas kernels for 0%

commit v1 on v0

--- a/solution.py
+++ b/solution.py
@@ -181,7 +181,7 @@
     live_rows = (slot_rows < seq_count[0]).astype(jnp.float32)
     grad_out = cotangent.astype(jnp.float32) * live_rows[:, None]
     grad_low = grad_out.astype(jnp.bfloat16)
-    down_grad = jnp.einsum("rf,rd->fd", activ_low, grad_low, preferred_element_type=jnp.float32)
+    down_grad = jnp.einsum("rf,rd->df", activ_low, grad_low, preferred_element_type=jnp.float32)
     grad_activ = jnp.dot(grad_low, down_weight.T, preferred_element_type=jnp.float32)
     grad_upper = gate_pull(grad_activ)[0].astype(jnp.bfloat16)
     up_grad = jnp.einsum(
@@ -193,7 +193,7 @@
     grad_mixed = grad_out + grad_mixed_norm
     grad_attn_low = grad_mixed.astype(jnp.bfloat16)
     out_grad = jnp.einsum(
-        "rh,rd->hd", attended_low, grad_attn_low, preferred_element_type=jnp.float32
+        "rh,rd->dh", attended_low, grad_attn_low, preferred_element_type=jnp.float32
     )
     grad_heads = jnp.dot(grad_attn_low, out_weight.T, preferred_element_type=jnp.float32).astype(
         jnp.bfloat16
@@ -223,29 +223,19 @@
     first_grad = lax.psum_scatter(first_part, "tensor", scatter_dimension=1, tiled=True)
     grad_in_norm, gain1_grad, shift1_grad = pull_one(grad_one)
     input_grad = grad_mixed + grad_in_norm
-    (
-        gain1_total,
-        shift1_total,
-        query_total,
-        key_total,
-        value_total,
-        out_total,
-        gain2_total,
-        shift2_total,
-        up_total,
-        down_total,
-    ) = (
-        lax.psum_scatter(gain1_grad, "dp", scatter_dimension=0, tiled=True),
-        lax.psum_scatter(shift1_grad, "dp", scatter_dimension=0, tiled=True),
-        lax.psum_scatter(query_grad, "dp", scatter_dimension=0, tiled=True),
-        lax.psum_scatter(key_grad, "dp", scatter_dimension=0, tiled=True),
-        lax.psum_scatter(value_grad, "dp", scatter_dimension=0, tiled=True),
-        lax.psum_scatter(out_grad, "dp", scatter_dimension=1, tiled=True),
-        lax.psum_scatter(gain2_grad, "dp", scatter_dimension=0, tiled=True),
-        lax.psum_scatter(shift2_grad, "dp", scatter_dimension=0, tiled=True),
-        lax.psum_scatter(up_grad, "dp", scatter_dimension=0, tiled=True),
-        lax.psum_scatter(down_grad, "dp", scatter_dimension=1, tiled=True),
-    )
+    columns = [query_grad, key_grad, value_grad, out_grad, up_grad, down_grad]
+    widths = [part.shape[1] for part in columns]
+    vectors = jnp.stack([gain1_grad, shift1_grad, gain2_grad, shift2_grad], axis=1)
+    vectors = jnp.pad(vectors, ((0, 0), (0, 124)))
+    packed = jnp.concatenate(columns + [vectors], axis=1)
+    summed = lax.psum_scatter(packed, "dp", scatter_dimension=0, tiled=True)
+    pieces, start = [], 0
+    for width in widths:
+        pieces.append(summed[:, start : start + width])
+        start += width
+    query_total, key_total, value_total, out_rows, up_total, down_rows = pieces
+    out_total, down_total = out_rows.T, down_rows.T
+    gain1_total, shift1_total, gain2_total, shift2_total = (summed[:, start + n] for n in range(4))
     return (
         layer_out,
         input_grad,

time: 1380 us -> 835 us (0.61)
  waiting for transfers between devices: 753 us -> 270 us
  blocking collectives: 77.1 us -> 0 us
  local copies, waits for them, and re-layouts: 209 us -> 231 us
    reduce_scatter x6 -> x1, waiting for transfers between devices: 686 us -> 196 us  [on_device(): summed = lax.psum_scatter(packed, 'dp', scatter_dimension=0, tiled=True)]
    unnamed x1 -> x0, blocking collectives: 77.1 us -> none
    concatenate x0 -> x1, local copies, waits for them, and re-layouts: none -> 16.4 us  [on_device(): packed = jnp.concatenate(columns + [vectors], axis=1)]
  transfers between devices with their start and end apart: 10 -> 5, of which waited for: 9 -> 5; matrix products, arithmetic and copies ran while one was open for 7% -> 10% of each run, Pallas kernels for 0% -> 0%
where the time goes in v1:
time: 835 us; the launch traced here: 820 us
  waiting for transfers between devices  270 us (32%)
  local copies, waits for them, and re-layouts  231 us (28%)
  matrix products  203 us (24%)
  other arithmetic  97.2 us (12%)
  between operations  15.7 us (2%)
    reduce_scatter x1, waiting for transfers between devices, on_device(): summed = lax.psum_scatter(packed, 'dp', scatter_dimension=0, tiled=True)  196 us
    dynamic_update_slice x4, local copies, waits for them, and re-layouts, attend_backward(): lax.map(one_sequence, (queries, keys_low, values, grad_heads, peaks_all,...  58.6 us
    dot_general x8, matrix products, causal_scores(): jnp.einsum('qhd,khd->hqk', query_block, seq_keys, preferred_element_type=...  37.4 us
    psum x1, waiting for transfers between devices, on_device(): mixed = inputs + lax.psum(attn_part, 'tensor')  33.7 us
    psum x1, waiting for transfers between devices, on_device(): grad_two = lax.psum(two_part, 'tensor')  19.8 us
    dot_general x4, matrix products, one_block(): jnp.einsum('hqk,khd->qhd', weights_low, seq_values, preferred_element_typ...  17.7 us
  transfers between devices with their start and end apart: 5, of which 5 were waited for; matrix products, arithmetic and copies ran while one was open for 10% of the time, Pallas kernels for 0%

profile of v1, /device:TPU:0, one launch (start us, length us, event | category | flops | bytes accessed | tf_op | source)
XLA Modules:
  0.0 819.7 jit_solution(13524710912855418834)
XLA Ops:
  29.6 4.6 pad_maximum_fusion
  48.4 4.8 convolution_convert_fusion.2
  65.5 86.7 %while.58 = (s32[]{:T(128)}, bf16[2,1024,6,64]{3,2,1,0:T(8,128)(2,1)}, f32[2,2,6,512]{3,2,1,0:T(8,128)}, f32[2,2,6,512]{3,2,1,0:T(8,128)S(1)}, bf16[2,1024,6,64]...) while((s32[]{:T(128)}, ...), condition=%wide.region_7.8_spmd, body=%wide.region_2.7_spmd.sunk | while | flops 843770368 | bytes 65536428 | solution.py:65
  73.6 28.0 %while.61 = (s32[]{:T(128)}, bf16[2,512,6,64]{1,3,2,0:T(8,128)(2,1)}, f32[2,6,512]{2,1,0:T(8,128)S(1)}, f32[2,6,512]{2,1,0:T(8,128)S(1)}, s32[2]{0:T(128)S(1)}, ...) while((s32[]{:T(128)}, ...), condition=%wide.region_6.6_spmd, body=%wide.region_3.5_spmd.sunk | while | flops 843770368 | bytes 51781844 | solution.py:62
  116.9 28.0 %while.61 = (s32[]{:T(128)}, bf16[2,512,6,64]{1,3,2,0:T(8,128)(2,1)}, f32[2,6,512]{2,1,0:T(8,128)S(1)}, f32[2,6,512]{2,1,0:T(8,128)S(1)}, s32[2]{0:T(128)S(1)}, ...) while((s32[]{:T(128)}, ...), condition=%wide.region_6.6_spmd, body=%wide.region_3.5_spmd.sunk | while | flops 843770368 | bytes 51781844 | solution.py:62
  152.2 6.1 reshape.234
  158.3 6.0 fusion.76
  165.4 33.7 %all-reduce.6.cloned.1.call-done = f32[2048,768]{1,0:T(8,128)} async-done(((f32[2048,768]{1,0:T(8,128)}), f32[2048,768]{1,0:T(8,128)}) %all-reduce.6.cloned.1.call-update) | async-done | bytes 6291472 | tf_op jit(solution)/shard_map/psum | solution.py:172
  206.3 8.3 %fusion.72 = f32[2048,1536]{1,0:T(8,128)} fusion(bf16[768,1536]{1,0:T(8,128)(2,1)S(1)} %copy-done, f32[2048,768]{1,0:T(8,128)S(1)} %get-tuple-element.427, f32[768]{0:T(1024)S(1)} %copy-done.75, f32[768]{0:T(1024)S(1)} %copy-done.68, f32[2048]{0:T(1024)S(1)} %fusion.64, f32[2048]{0:T(1024)S(1)} %broadcast_multiply_fusion), kind=kOutput, calls=%fused_computation.143 | convolution fusion | flops 4839702528 | bytes 21256192 | tf_op jit(solution)/shard_map/dot_general | solution.py:175
  214.6 13.7 %fusion.38 = bf16[2048,1536]{1,0:T(8,128)(2,1)S(1)} fusion(f32[2048,1536]{1,0:T(8,128)} %fusion.72, bf16[1536,768]{1,0:T(8,128)(2,1)S(1)} %copy-done.73, bf16[2048,768]{1,0:T(8,128)(2,1)S(1)} %copy-done.23, f32[2048]{0:T(1024)S(1)} %fusion.62), kind=kOutput, calls=%fused_computation.71 | convolution fusion | flops 4899471360 | bytes 24387584 | tf_op jit(solution)/shard_map/dot_general | solution.py:185
  231.0 6.9 fusion.77
  239.5 12.0 %fusion.73 = f32[2048,768]{1,0:T(8,128)} fusion(bf16[1536,768]{1,0:T(8,128)(2,1)S(1)} %copy-done.74, f32[2048,1536]{1,0:T(8,128)} %fusion.72), kind=kOutput, calls=%fused_computation.144 | convolution fusion | flops 4860149760 | bytes 21233664 | tf_op jit(solution)/shard_map/dot_general | solution.py:178
  251.5 19.8 %all-reduce.8.cloned.1.call-done = f32[2048,768]{1,0:T(8,128)} async-done(((f32[2048,768]{1,0:T(8,128)}), f32[2048,768]{1,0:T(8,128)}) %all-reduce.8.cloned.1.call-update) | async-done | bytes 6291472 | tf_op jit(solution)/shard_map/psum | solution.py:191
  271.3 6.4 multiply_reduce_fusion.1
  294.4 185.6 %while.60 = (s32[]{:T(128)}, bf16[2,1024,6,64]{3,2,1,0:T(8,128)(2,1)}, bf16[2,1024,6,64]{1,3,2,0:T(8,128)(2,1)}, f32[2,1024,6,64]{1,0,3,2:T(2,128)}, bf16[2,1024...) while((s32[]{:T(128)}, ...), condition=%wide.region_19.20_spmd, body=%wide.region_15.19_spmd.sunk | while | flops 2047997440 | bytes 193598400 | solution.py:120
  303.0 45.7 %while.62 = (s32[]{:T(128)}, f32[1024,6,64]{0,2,1:T(8,128)}, f32[1024,6,64]{0,2,1:T(8,128)}, bf16[2,512,6,64]{1,3,2,0:T(8,128)(2,1)}, bf16[2,512,6,64]{1,3,2,0:T...) while((s32[]{:T(128)}, f32[1024,6,64]{0,2,1:T(8,128)}, ...), condition=%wide.region_18.18_spmd.clone, body=%wide.region_16.17_spmd.clone.sunk | while | flops 2047604224 | bytes 159814224 | solution.py:107
  307.7 6.0 multiply_reduce_fusion.5
  329.7 6.0 multiply_reduce_fusion.5
  356.3 27.7 %dynamic_update_slice.59 = f32[2,1024,6,64]{1,0,3,2:T(2,128)} dynamic-update-slice(f32[2,1024,6,64]{1,0,3,2:T(2,128)} %get-tuple-element.866, f32[1,1024,6,64]{1,0,3,2:T(1,128)S(1)} %copy.145, s32[]{:T(128)S(6)} %copy.198, s32[]{:T(128)} %constant.119.clone.1..sunk.1, s32[]{:T(128)} %constant.119.clone.1..sunk.1, s32[]{:T(128)} %constant.119.clone.1..sunk.1) | dynamic-update-slice | bytes 3145732 | tf_op jit(solution)/shard_map/while/body/jit(dynamic_update_index_in_dim)/dynamic_update_slice | solution.py:120
  395.5 45.7 %while.62 = (s32[]{:T(128)}, f32[1024,6,64]{0,2,1:T(8,128)}, f32[1024,6,64]{0,2,1:T(8,128)}, bf16[2,512,6,64]{1,3,2,0:T(8,128)(2,1)}, bf16[2,512,6,64]{1,3,2,0:T...) while((s32[]{:T(128)}, f32[1024,6,64]{0,2,1:T(8,128)}, ...), condition=%wide.region_18.18_spmd.clone, body=%wide.region_16.17_spmd.clone.sunk | while | flops 2047604224 | bytes 159814224 | solution.py:107
  400.2 6.0 multiply_reduce_fusion.5
  422.2 6.0 multiply_reduce_fusion.5
  448.8 27.7 %dynamic_update_slice.59 = f32[2,1024,6,64]{1,0,3,2:T(2,128)} dynamic-update-slice(f32[2,1024,6,64]{1,0,3,2:T(2,128)} %get-tuple-element.866, f32[1,1024,6,64]{1,0,3,2:T(1,128)S(1)} %copy.145, s32[]{:T(128)S(6)} %copy.198, s32[]{:T(128)} %constant.119.clone.1..sunk.1, s32[]{:T(128)} %constant.119.clone.1..sunk.1, s32[]{:T(128)} %constant.119.clone.1..sunk.1) | dynamic-update-slice | bytes 3145732 | tf_op jit(solution)/shard_map/while/body/jit(dynamic_update_index_in_dim)/dynamic_update_slice | solution.py:120
  486.2 5.3 reshape.235
  501.9 13.4 %fusion.71 = f32[768,1536]{1,0:T(8,128)} fusion(bf16[2048,1536]{1,0:T(8,128)(2,1)} %copy-done.79, f32[2048,768]{1,0:T(8,128)} %copy-done.8, f32[768]{0:T(1024)S(1)} %copy-done.76, f32[768]{0:T(1024)S(1)} %copy-done.69, f32[2048]{0:T(1024)S(1)} %copy-done.63, f32[2048]{0:T(1024)S(1)} %copy-done.55), kind=kOutput, calls=%fused_computation.142 | convolution fusion | flops 4839702528 | bytes 17324032 | tf_op jit(solution)/shard_map/rd,rf->df/dot_general | solution.py:187
  515.3 12.9 %fusion.55 = f32[768,1536]{1,0:T(8,128)} fusion(bf16[2048,768]{1,0:T(8,128)(2,1)S(1)} %copy-done.25, f32[2048]{0:T(1024)S(1)} %copy-done.57, f32[2048,1536]{1,0:T(8,128)} %fusion.72), kind=kOutput, calls=%fused_computation.110 | convolution fusion | flops 4864868352 | bytes 20455424 | tf_op jit(solution)/shard_map/rf,rd->df/dot_general | solution.py:184
  538.7 13.3 %all-reduce.10.cloned.1.call-done = (f32[2048,768]{1,0:T(8,128)}, f32[2048,768]{1,0:T(8,128)}) async-done(((f32[2048,768]{1,0:T(8,128)}, f32[2048,768]{1,0:T(8,128)}), (f32[2048,768]{1,0:T(8,128)}, f32[2048,768]{1,0:T(8,128)})) %all-reduce.10.cloned.1.call-update) | async-done | bytes 12582928 | tf_op jit(solution)/shard_map/psum | solution.py:179
  560.6 16.4 %concatenate.14 = f32[768,4544]{1,0:T(8,128)} concatenate(f32[768,384]{1,0:T(8,128)} %fusion.80, f32[768,384]{1,0:T(8,128)} %fusion.81, f32[768,192]{1,0:T(8,128)} %fusion.82, f32[768,384]{1,0:T(8,128)} %fusion.83, f32[768,1536]{1,0:T(8,128)} %fusion.71, f32[768,1536]{1,0:T(8,128)} %fusion.55, f32[768,128]{1,0:T(8,128)S(1)} %pad.4), dimensions={1} | concatenate | bytes 27918336 | tf_op jit(solution)/shard_map/concatenate | solution.py:230
  585.2 8.8 %add.127 = f32[2048,768]{1,0:T(8,128)} add(f32[2048,768]{1,0:T(8,128)} %copy-done.8, f32[2048,768]{1,0:T(8,128)} %get-tuple-element.422) | non-fusion elementwise | flops 1572864 | bytes 18874368 | tf_op jit(solution)/shard_map/add | solution.py:179
  594.1 8.9 %add_add_fusion.2 = f32[2048,768]{1,0:T(8,128)} fusion(f32[2048,768]{1,0:T(8,128)} %copy-done.12, bf16[2048,768]{1,0:T(8,128)(2,1)S(1)} %copy-done.26, f32[2048]{0:T(1024)S(1)} %negate_multiply_fusion, f32[2048]{0:T(1024)S(1)} %copy-done.59, f32[2048]{0:T(1024)S(1)} %copy-done.57, f32[2048]{0:T(1024)S(1)} %multiply_multiply_fusion.2, ...), kind=kLoop, calls=%fused_computation.90 | loop fusion | flops 20447232 | bytes 25218048 | tf_op jit(solution)/shard_map/add | solution.py:225
  603.0 196.5 %reduce-scatter.5.cloned.1.call-done = f32[48,4544]{1,0:T(8,128)} async-done(((f32[768,4544]{1,0:T(8,128)}), f32[48,4544]{1,0:T(8,128)}) %reduce-scatter.5.cloned.1.call-update) | async-done | bytes 872464 | tf_op jit(solution)/shard_map/reduce_scatter | solution.py:231
  806.4 6.4 reduce-scatter.3.cloned.1.call-done
  (451 shorter events, 319.1 us)
Async XLA Ops:
  7.2 199.1 %copy-start = (bf16[768,1536]{1,0:T(8,128)(2,1)S(1)}, bf16[768,1536]{1,0:T(8,128)(2,1)}, u32[]{:S(2)}) copy-start(bf16[768,1536]{1,0:T(8,128)(2,1)} %param.35) | copy-start | bytes 7077892
  7.2 192.0 %all-reduce.6.cloned.1.call-start = ((), (), s32[]{:S(2)}) async-start(), calls=%async_computation.2 | async-start | bytes 12582912 | tf_op jit(solution)/shard_map/psum | solution.py:172
  9.8 10.0 %copy-start.64 = (f32[768]{0:T(1024)S(1)}, f32[768]{0:T(1024)}, u32[]{:S(2)}) copy-start(f32[768]{0:T(1024)} %param.27) | copy-start | bytes 9220
  9.8 10.0 %copy-start.70 = (f32[768]{0:T(1024)S(1)}, f32[768]{0:T(1024)}, u32[]{:S(2)}) copy-start(f32[768]{0:T(1024)} %param.28) | copy-start | bytes 9220
  9.8 12.8 %copy-start.50 = (f32[2048]{0:T(1024)}, f32[2048]{0:T(1024)S(1)}, u32[]{:S(2)}) copy-start(f32[2048]{0:T(1024)S(1)} %broadcast_multiply_fusion.1) | copy-start | bytes 24580
  12.8 9.8 %copy-start.52 = (f32[2048]{0:T(1024)}, f32[2048]{0:T(1024)S(1)}, u32[]{:S(2)}) copy-start(f32[2048]{0:T(1024)S(1)} %fusion.63) | copy-start | bytes 24580
  19.8 9.8 %copy-start.39 = (bf16[2,1024,3,64]{1,0,2,3:T(2,128)(2,1)S(1)}, bf16[2,1024,3,64]{1,0,2,3:T(2,128)(2,1)}, u32[]{:S(2)}) copy-start(bf16[2,1024,3,64]{1,0,2,3:T(2,128)(2,1)} %reshape.233) | copy-start | bytes 2359300
  38.8 9.6 %copy-start.42 = (bf16[768,384]{1,0:T(8,128)(2,1)S(1)}, bf16[768,384]{1,0:T(8,128)(2,1)}, u32[]{:S(2)}) copy-start(bf16[768,384]{1,0:T(8,128)(2,1)} %param.29) | copy-start | bytes 1769476
  164.3 107.0 %all-reduce.8.cloned.1.call-start = ((), (), s32[]{:S(2)}) async-start(), calls=%async_computation.3 | async-start | bytes 12582912 | tf_op jit(solution)/shard_map/psum | solution.py:191
  165.4 116.8 %copy-start.56 = (f32[2048]{0:T(1024)}, f32[2048]{0:T(1024)S(1)}, u32[]{:S(2)}) copy-start(f32[2048]{0:T(1024)S(1)} %fusion.62) | copy-start | bytes 24580
  203.6 74.1 %copy-start.54 = (f32[2048]{0:T(1024)}, f32[2048]{0:T(1024)S(1)}, u32[]{:S(2)}) copy-start(f32[2048]{0:T(1024)S(1)} %broadcast_multiply_fusion) | copy-start | bytes 24580
  206.3 71.5 %copy-start.62 = (f32[2048]{0:T(1024)}, f32[2048]{0:T(1024)S(1)}, u32[]{:S(2)}) copy-start(f32[2048]{0:T(1024)S(1)} %fusion.64) | copy-start | bytes 24580
  237.9 314.1 %all-reduce.10.cloned.1.call-start = ((), (), s32[]{:S(2)}) async-start(), calls=%async_computation.6 | async-start | bytes 25165824 | tf_op jit(solution)/shard_map/psum | solution.py:179
  352.3 35.0 %copy-start.47 = (f32[2,2,6,512]{3,2,1,0:T(8,128)S(1)}, f32[2,2,6,512]{3,2,1,0:T(8,128)}, u32[]{:S(2)}) copy-start(f32[2,2,6,512]{3,2,1,0:T(8,128)} %copy-done.46) | copy-start | bytes 147460 | tf_op jit(solution)/shard_map/while
  444.7 35.1 %copy-start.47 = (f32[2,2,6,512]{3,2,1,0:T(8,128)S(1)}, f32[2,2,6,512]{3,2,1,0:T(8,128)}, u32[]{:S(2)}) copy-start(f32[2,2,6,512]{3,2,1,0:T(8,128)} %copy-done.46) | copy-start | bytes 147460 | tf_op jit(solution)/shard_map/while
  501.2 14.1 %copy-start.25 = (bf16[2048,768]{1,0:T(8,128)(2,1)S(1)}, bf16[2048,768]{1,0:T(8,128)(2,1)}, u32[]{:S(2)}) copy-start(bf16[2048,768]{1,0:T(8,128)(2,1)} %param.37) | copy-start | bytes 9437188
  501.2 14.1 %copy-start.57 = (f32[2048]{0:T(1024)S(1)}, f32[2048]{0:T(1024)}, u32[]{:S(2)}) copy-start(f32[2048]{0:T(1024)} %copy-done.56) | copy-start | bytes 24580
  501.2 298.3 %reduce-scatter.5.cloned.1.call-start = ((), (), s32[]{:S(2)}) async-start(), calls=%async_computation.5 | async-start | bytes 15040512 | tf_op jit(solution)/shard_map/reduce_scatter | solution.py:231
  515.3 12.9 %copy-start.67 = (f32[768]{0:T(1024)S(1)}, f32[768]{0:T(1024)}, u32[]{:S(2)}) copy-start(f32[768]{0:T(1024)} %get-tuple-element.340) | copy-start | bytes 9220
  515.3 12.9 %copy-start.66 = (f32[768]{0:T(1024)S(1)}, f32[768]{0:T(1024)}, u32[]{:S(2)}) copy-start(f32[768]{0:T(1024)} %get-tuple-element.345) | copy-start | bytes 9220
  515.3 12.9 %copy-start.29 = (bf16[2048,768]{1,0:T(8,128)(2,1)S(1)}, bf16[2048,768]{1,0:T(8,128)(2,1)}, u32[]{:S(2)}) copy-start(bf16[2048,768]{1,0:T(8,128)(2,1)} %copy-done.27) | copy-start | bytes 9437188
  515.3 12.9 %copy-start.38 = (bf16[2048,3,64]{0,2,1:T(8,128)(2,1)S(1)}, bf16[2048,3,64]{0,2,1:T(8,128)(2,1)}, u32[]{:S(2)}) copy-start(bf16[2048,3,64]{0,2,1:T(8,128)(2,1)} %slice.68) | copy-start | bytes 2359300
  515.3 14.9 %copy-start.36 = (bf16[48,8,2,1024]{3,1,2,0:T(8,128)(2,1)S(1)}, bf16[48,8,2,1024]{3,1,2,0:T(8,128)(2,1)}, u32[]{:S(2)}) copy-start(bf16[48,8,2,1024]{3,1,2,0:T(8,128)(2,1)} %copy-done.35) | copy-start | bytes 4718596
  533.0 19.0 %copy-start.9 = (bf16[2048,768]{1,0:T(8,128)(2,1)S(1)}, bf16[2048,768]{1,0:T(8,128)(2,1)}, u32[]{:S(2)}) copy-start(bf16[2048,768]{1,0:T(8,128)(2,1)} %param.23) | copy-start | bytes 9437188
  533.0 19.0 %copy-start.51 = (f32[2048]{0:T(1024)S(1)}, f32[2048]{0:T(1024)}, u32[]{:S(2)}) copy-start(f32[2048]{0:T(1024)} %copy-done.50) | copy-start | bytes 24580
  533.0 19.0 %copy-start.65 = (f32[768]{0:T(1024)S(1)}, f32[768]{0:T(1024)}, u32[]{:S(2)}) copy-start(f32[768]{0:T(1024)} %param.27) | copy-start | bytes 9220
  535.9 20.3 %copy-start.61 = (f32[2048]{0:T(1024)S(1)}, f32[2048]{0:T(1024)}, u32[]{:S(2)}) copy-start(f32[2048]{0:T(1024)} %copy-done.60) | copy-start | bytes 24580
  535.9 20.3 %copy-start.53 = (f32[2048]{0:T(1024)S(1)}, f32[2048]{0:T(1024)}, u32[]{:S(2)}) copy-start(f32[2048]{0:T(1024)} %copy-done.52) | copy-start | bytes 24580
  577.0 235.7 %reduce-scatter.3.cloned.1.call-start = ((), (), s32[]{:S(2)}) async-start(), calls=%async_computation.4 | async-start | bytes 4718592 | tf_op jit(solution)/shard_map/reduce_scatter | solution.py:223
  585.2 8.8 %copy-start.10 = (bf16[2048,768]{1,0:T(8,128)(2,1)S(1)}, bf16[2048,768]{1,0:T(8,128)(2,1)}, u32[]{:S(2)}) copy-start(bf16[2048,768]{1,0:T(8,128)(2,1)} %param.23) | copy-start | bytes 9437188
  585.2 8.8 %copy-start.26 = (bf16[2048,768]{1,0:T(8,128)(2,1)S(1)}, bf16[2048,768]{1,0:T(8,128)(2,1)}, u32[]{:S(2)}) copy-start(bf16[2048,768]{1,0:T(8,128)(2,1)} %param.37) | copy-start | bytes 9437188
  594.1 218.7 %copy-start.1 = (bf16[768,1536]{1,0:T(8,128)(2,1)S(1)}, bf16[768,1536]{1,0:T(8,128)(2,1)}, u32[]{:S(2)}) copy-start(bf16[768,1536]{1,0:T(8,128)(2,1)} %param.35) | copy-start | bytes 7077892
  (102 other events, 338.0 us)
Sparse Core Ops, SparseCore 0:
  164.4 34.7 all-reduce.5
  238.0 33.2 all-reduce.7
  501.3 50.6 all-reduce.9
  577.2 222.2 reduce-scatter.4
  802.2 10.4 reduce-scatter.2

commit v2 on v1

v2 whole, which is shorter than its diff:
```python
import functools

import jax
import jax.numpy as jnp
from jax import lax
from jax.experimental import pallas as pl
from jax.experimental.pallas import tpu as pltpu
from jax.sharding import PartitionSpec as P

HEAD_DIM = 64
SEQ_LEN = 1024
BLOCK = 256
PAIR = 2 * HEAD_DIM
EPS = 1e-05
FILL = -1e30
VMEM_BYTES = 60 * 1024 * 1024

F32 = jnp.float32
BF16 = jnp.bfloat16


def dot_nn(left, right):
    return lax.dot_general(left, right, (((1,), (0,)), ((), ())), preferred_element_type=F32)


def dot_nt(left, right):
    return lax.dot_general(left, right, (((1,), (1,)), ((), ())), preferred_element_type=F32)


def norm_stats(values_in):
    average = jnp.mean(values_in, axis=-1, keepdims=True)
    centered = values_in - average
    variance = jnp.mean(centered * centered, axis=-1, keepdims=True)
    factor = lax.rsqrt(variance + EPS)
    return centered * factor, factor


def norm_backward(grad, normed, factor, gain):
    scaled = grad * gain
    mean_plain = jnp.mean(scaled, axis=-1, keepdims=True)
    mean_cross = jnp.mean(scaled * normed, axis=-1, keepdims=True)
    return factor * (scaled - mean_plain - normed * mean_cross)


def head_masks(rows):
    lanes = lax.broadcasted_iota(jnp.int32, (rows, PAIR), 1)
    return lanes < HEAD_DIM


def split_heads(pair_rows):
    first = head_masks(pair_rows.shape[0])
    zero = jnp.zeros_like(pair_rows)
    return jnp.where(first, pair_rows, zero), jnp.where(first, zero, pair_rows)


def front_kernel(
    scal,
    x_ref,
    fv_ref,
    gain_ref,
    shift_ref,
    wq_own,
    wk_own,
    wv_own,
    wq_peer,
    wk_peer,
    wv_peer,
    sel_ref,
    n1_ref,
    q_ref,
    k_ref,
    v_ref,
    att_ref,
    lse_ref,
    w_scr,
    lse_scr,
):
    step = pl.program_id(0)
    length = x_ref.shape[0]
    blocks = length // BLOCK
    half = pl.num_programs(0) // 2

    @pl.when(step == 0)
    def _():
        lse_scr[...] = jnp.zeros_like(lse_scr)

        def one(row, carry):
            rows = pl.ds(row * BLOCK, BLOCK)
            normed, _ = norm_stats(x_ref[rows, :].astype(F32))
            n1_ref[rows, :] = (normed * gain_ref[...] + shift_ref[...]).astype(BF16)
            return carry

        lax.fori_loop(0, blocks, one, 0)

    @pl.when(step < half)
    def _():
        w_scr[:, 0:PAIR] = wq_own[...]
        w_scr[:, PAIR : 2 * PAIR] = wk_own[...]
        w_scr[:, 2 * PAIR : 3 * PAIR] = wv_own[...]

    @pl.when(step >= half)
    def _():
        w_scr[:, 0:PAIR] = wq_peer[...].astype(BF16)
        w_scr[:, PAIR : 2 * PAIR] = wk_peer[...].astype(BF16)
        w_scr[:, 2 * PAIR : 3 * PAIR] = wv_peer[...].astype(BF16)

    for block in range(blocks):
        rows = slice(block * BLOCK, (block + 1) * BLOCK)
        fused = dot_nn(n1_ref[rows, :], w_scr[...])
        picked = dot_nn(fv_ref[rows, :], sel_ref[...])
        q_ref[rows, :] = (fused[:, 0:PAIR].astype(BF16).astype(F32) * HEAD_DIM**-0.5).astype(BF16)
        k_ref[rows, :] = fused[:, PAIR : 2 * PAIR].astype(BF16)
        v_ref[rows, :] = (fused[:, 2 * PAIR :] + picked).astype(BF16)

    lane = lax.broadcasted_iota(jnp.int32, (BLOCK, PAIR), 1)
    row_pos = lax.broadcasted_iota(jnp.int32, (BLOCK, BLOCK), 0)
    col_pos = lax.broadcasted_iota(jnp.int32, (BLOCK, BLOCK), 1)
    seen = col_pos <= row_pos
    for block in range(blocks):
        lo, hi = block * BLOCK, (block + 1) * BLOCK
        queries = split_heads(q_ref[lo:hi, :])
        total = jnp.zeros((BLOCK, PAIR), F32)
        lse_tile = lse_scr[lo:hi, :]
        for head in range(2):
            diag = jnp.where(seen, dot_nt(queries[head], k_ref[lo:hi, :]), FILL)
            peak = jnp.max(diag, axis=-1, keepdims=True)
            if block:
                early = dot_nt(queries[head], k_ref[0:lo, :])
                peak = jnp.maximum(peak, jnp.max(early, axis=-1, keepdims=True))
            diag = jnp.exp(diag - peak)
            mass = jnp.sum(diag, axis=-1, keepdims=True)
            if block:
                early = jnp.exp(early - peak)
                mass = mass + jnp.sum(early, axis=-1, keepdims=True)
            inverse = 1.0 / mass
            total = total + dot_nn((diag * inverse).astype(BF16), split_heads(v_ref[lo:hi, :])[head])
            if block:
                total = total + dot_nn(
                    (early * inverse).astype(BF16), split_heads(v_ref[0:lo, :])[head]
                )
            lse_tile = jnp.where(lane == 2 * step + head, peak + jnp.log(mass), lse_tile)
        att_ref[lo:hi, :] = total.astype(BF16)
        lse_scr[lo:hi, :] = lse_tile

    @pl.when(step == pl.num_programs(0) - 1)
    def _():
        for block in range(blocks):
            lo, hi = block * BLOCK, (block + 1) * BLOCK
            lse_ref[:, lo:hi] = jnp.transpose(lse_scr[lo:hi, :])[0 : lse_ref.shape[0], :]


def front(scal, tokens, first_values, gain, shift, own, peer, select):
    width = tokens.shape[1]
    own_width = own[0].shape[1]
    heads_width = 2 * own_width
    half = own_width // PAIR
    fv_width = first_values.shape[1]
    row_block = lambda i, s: (s[0], 0)
    whole = lambda i, s: (0, 0)
    own_block = pl.BlockSpec((width, PAIR), lambda i, s: (0, jnp.minimum(i, half - 1)))
    peer_block = pl.BlockSpec((width, PAIR), lambda i, s: (0, jnp.maximum(i - half, 0)))
    pair_block = pl.BlockSpec((SEQ_LEN, PAIR), lambda i, s: (0, i))
    pair_out = jax.ShapeDtypeStruct((SEQ_LEN, heads_width), BF16)
    return pl.pallas_call(
        front_kernel,
        grid_spec=pltpu.PrefetchScalarGridSpec(
            num_scalar_prefetch=1,
            grid=(2 * half,),
            in_specs=[
                pl.BlockSpec((SEQ_LEN, width), row_block),
                pl.BlockSpec((SEQ_LEN, fv_width), row_block),
                pl.BlockSpec((1, width), whole),
                pl.BlockSpec((1, width), whole),
                own_block,
                own_block,
                own_block,
                peer_block,
                peer_block,
                peer_block,
                pl.BlockSpec((fv_width, PAIR), lambda i, s: (0, i)),
            ],
            out_specs=[
                pl.BlockSpec((SEQ_LEN, width), whole),
                pair_block,
                pair_block,
                pair_block,
                pair_block,
                pl.BlockSpec((16, SEQ_LEN), whole),
            ],
            scratch_shapes=[
                pltpu.VMEM((width, 3 * PAIR), BF16),
                pltpu.VMEM((SEQ_LEN, PAIR), F32),
            ],
        ),
        out_shape=[
            jax.ShapeDtypeStruct((SEQ_LEN, width), BF16),
            pair_out,
            pair_out,
            pair_out,
            pair_out,
            jax.ShapeDtypeStruct((16, SEQ_LEN), F32),
        ],
        compiler_params=pltpu.CompilerParams(vmem_limit_bytes=VMEM_BYTES),
        name="front",
    )(scal, tokens, first_values, gain, shift, *own, *peer, select)


def gelu_pair(upper):
    scale = (2.0 / jnp.pi) ** 0.5
    square = upper * upper
    inner = upper * (scale + (scale * 0.044715) * square)
    tanh = jnp.tanh(inner)
    cdf = 0.5 + 0.5 * tanh
    slope = cdf + 0.5 * upper * (1.0 - tanh * tanh) * (scale + (3.0 * scale * 0.044715) * square)
    return upper * cdf, slope


def middle_kernel(
    scal,
    x_ref,
    att_ref,
    cot_ref,
    gain_ref,
    shift_ref,
    wo_own,
    wo_peer,
    up_own,
    down_own,
    up_peer,
    down_peer,
    layer_ref,
    gmix_ref,
    gheads_ref,
    og_own,
    og_peer,
    ug_own,
    dg_own,
    ug_peer,
    dg_peer,
    vec_ref,
    mixed_scr,
    two_scr,
    low_scr,
    two_t,
    low_t,
    act_scr,
    gup_scr,
    gtwo_scr,
    up_scr,
    down_scr,
    wo_scr,
):
    step = pl.program_id(0)
    length, width = x_ref.shape
    blocks = length // BLOCK
    own_width = wo_own.shape[0]

    @pl.when(step == 0)
    def _():
        wo_scr[0:own_width, :] = wo_own[...]
        wo_scr[own_width:, :] = wo_peer[...].astype(BF16)
        live = jnp.where(scal[1] > 0, 1.0, 0.0).astype(F32)
        for block in range(blocks):
            rows = slice(block * BLOCK, (block + 1) * BLOCK)
            mixed = x_ref[rows, :].astype(F32) + dot_nn(att_ref[rows, :], wo_scr[...])
            mixed_scr[rows, :] = mixed
            normed, _ = norm_stats(mixed)
            two = (normed * gain_ref[...] + shift_ref[...]).astype(BF16)
            two_scr[rows, :] = two
            two_t[:, rows] = jnp.transpose(two)
            low = (cot_ref[rows, :].astype(F32) * live).astype(BF16)
            low_scr[rows, :] = low
            low_t[:, rows] = jnp.transpose(low)
            layer_ref[rows, :] = mixed
            gtwo_scr[rows, :] = jnp.zeros_like(mixed)

    @pl.when(step % 2 == 0)
    def _():
        up_scr[...] = up_peer[...].astype(BF16)
        down_scr[...] = down_peer[...].astype(BF16)

    @pl.when(step % 2 == 1)
    def _():
        up_scr[...] = up_own[...]
        down_scr[...] = down_own[...]

    for block in range(blocks):
        rows = slice(block * BLOCK, (block + 1) * BLOCK)
        upper = dot_nn(two_scr[rows, :], up_scr[...])
        active, slope = gelu_pair(upper)
        active = active.astype(BF16)
        act_scr[rows, :] = active
        layer_ref[rows, :] += dot_nn(active, down_scr[...])
        grad_upper = (dot_nt(low_scr[rows, :], down_scr[...]) * slope).astype(BF16)
        gup_scr[rows, :] = grad_upper
        gtwo_scr[rows, :] += dot_nt(grad_upper, up_scr[...])

    down_grad = dot_nn(low_t[...], act_scr[...])
    up_grad = dot_nn(two_t[...], gup_scr[...])

    @pl.when(step % 2 == 0)
    def _():
        dg_peer[...] = down_grad
        ug_peer[...] = up_grad

    @pl.when(step % 2 == 1)
    def _():
        dg_own[...] = down_grad
        ug_own[...] = up_grad

    @pl.when(step == pl.num_programs(0) - 1)
    def _():
        gain_sum = jnp.zeros((1, width), F32)
        shift_sum = jnp.zeros((1, width), F32)
        for block in range(blocks):
            rows = slice(block * BLOCK, (block + 1) * BLOCK)
            normed, factor = norm_stats(mixed_scr[rows, :])
            grad_two = gtwo_scr[rows, :]
            gain_sum += jnp.sum(grad_two * normed, axis=0, keepdims=True)
            shift_sum += jnp.sum(grad_two, axis=0, keepdims=True)
            grad_mixed = low_scr[rows, :].astype(F32) + norm_backward(
                grad_two, normed, factor, gain_ref[...]
            )
            gmix_ref[rows, :] = grad_mixed
            grad_attn = grad_mixed.astype(BF16)
            low_t[:, rows] = jnp.transpose(grad_attn)
            gheads_ref[rows, :] = dot_nt(grad_attn, wo_scr[...]).astype(BF16)
        vec_ref[...] = jnp.zeros_like(vec_ref)
        vec_ref[0:1, :] = gain_sum
        vec_ref[1:2, :] = shift_sum
        og_own[...] = dot_nn(low_t[...], att_ref[:, 0:own_width])
        og_peer[...] = dot_nn(low_t[...], att_ref[:, own_width:])


def middle(scal, tokens, attended, cotangent, gain, shift, out_own, out_peer, ups, downs):
    width = tokens.shape[1]
    own_ff = ups[0].shape[1]
    own_width = out_own.shape[0]
    ff_block = 512
    steps = 2 * (own_ff // ff_block)
    row_block = pl.BlockSpec((SEQ_LEN, width), lambda i, s: (s[0], 0))
    fixed = lambda shape: pl.BlockSpec(shape, lambda i, s: (0, 0))
    up_block = pl.BlockSpec((width, ff_block), lambda i, s: (0, i // 2))
    down_block = pl.BlockSpec((ff_block, width), lambda i, s: (i // 2, 0))
    seq_f32 = jax.ShapeDtypeStruct((SEQ_LEN, width), F32)
    grad_f32 = jax.ShapeDtypeStruct((width, own_ff), F32)
    out_f32 = jax.ShapeDtypeStruct((width, own_width), F32)
    return pl.pallas_call(
        middle_kernel,
        grid_spec=pltpu.PrefetchScalarGridSpec(
            num_scalar_prefetch=1,
            grid=(steps,),
            in_specs=[
                row_block,
                fixed((SEQ_LEN, width)),
                row_block,
                fixed((1, width)),
                fixed((1, width)),
                fixed((own_width, width)),
                fixed((own_width, width)),
                up_block,
                down_block,
                up_block,
                down_block,
            ],
            out_specs=[
                fixed((SEQ_LEN, width)),
                fixed((SEQ_LEN, width)),
                fixed((SEQ_LEN, width)),
                fixed((width, own_width)),
                fixed((width, own_width)),
                up_block,
                up_block,
                up_block,
                up_block,
                fixed((8, width)),
            ],
            scratch_shapes=[
                pltpu.VMEM((SEQ_LEN, width), F32),
                pltpu.VMEM((SEQ_LEN, width), BF16),
                pltpu.VMEM((SEQ_LEN, width), BF16),
                pltpu.VMEM((width, SEQ_LEN), BF16),
                pltpu.VMEM((width, SEQ_LEN), BF16),
                pltpu.VMEM((SEQ_LEN, ff_block), BF16),
                pltpu.VMEM((SEQ_LEN, ff_block), BF16),
                pltpu.VMEM((SEQ_LEN, width), F32),
                pltpu.VMEM((width, ff_block), BF16),
                pltpu.VMEM((ff_block, width), BF16),
                pltpu.VMEM((2 * own_width, width), BF16),
            ],
        ),
        out_shape=[
            seq_f32,
            seq_f32,
            jax.ShapeDtypeStruct((SEQ_LEN, 2 * own_width), BF16),
            out_f32,
            out_f32,
            grad_f32,
            grad_f32,
            grad_f32,
            grad_f32,
            jax.ShapeDtypeStruct((8, width), F32),
        ],
        compiler_params=pltpu.CompilerParams(vmem_limit_bytes=VMEM_BYTES),
        name="middle",
    )(scal, tokens, attended, cotangent, gain, shift, out_own, out_peer, *ups, *downs)


def back_kernel(
    scal,
    x_ref,
    n1_ref,
    q_ref,
    k_ref,
    v_ref,
    att_ref,
    gheads_ref,
    lse_ref,
    gmix_ref,
    gain_ref,
    wq_own,
    wk_own,
    wv_own,
    wq_peer,
    wk_peer,
    wv_peer,
    sel_ref,
    gin_ref,
    fvg_ref,
    grads_ref,
    vec_ref,
    n1_t,
    w_scr,
    dk_acc,
    dv_acc,
    dq_t,
    stack_scr,
    one_acc,
    fv_acc,
):
    step = pl.program_id(0)
    length, width = x_ref.shape
    blocks = length // BLOCK
    half = pl.num_programs(0) // 2

    @pl.when(step == 0)
    def _():
        for block in range(blocks):
            rows = slice(block * BLOCK, (block + 1) * BLOCK)
            n1_t[:, rows] = jnp.transpose(n1_ref[rows, :])
        one_acc[...] = jnp.zeros_like(one_acc)
        fv_acc[...] = jnp.zeros_like(fv_acc)

    @pl.when(step < half)
    def _():
        w_scr[:, 0:PAIR] = wq_own[...]
        w_scr[:, PAIR : 2 * PAIR] = wk_own[...]
        w_scr[:, 2 * PAIR : 3 * PAIR] = wv_own[...]

    @pl.when(step >= half)
    def _():
        w_scr[:, 0:PAIR] = wq_peer[...].astype(BF16)
        w_scr[:, PAIR : 2 * PAIR] = wk_peer[...].astype(BF16)
        w_scr[:, 2 * PAIR : 3 * PAIR] = wv_peer[...].astype(BF16)

    k_t = jnp.transpose(k_ref[...])
    prod_t = jnp.transpose(gheads_ref[...].astype(F32) * att_ref[...].astype(F32))
    lse_pair = lse_ref[0]
    row_pos = lax.broadcasted_iota(jnp.int32, (BLOCK, BLOCK), 0)
    col_pos = lax.broadcasted_iota(jnp.int32, (BLOCK, BLOCK), 1)
    seen = row_pos <= col_pos
    for block in range(blocks):
        cols = slice(block * BLOCK, (block + 1) * BLOCK)
        queries = split_heads(q_ref[cols, :])
        grads = split_heads(gheads_ref[cols, :])
        for head in range(2):
            part = slice(head * HEAD_DIM, (head + 1) * HEAD_DIM)
            delta = jnp.sum(prod_t[part, cols], axis=0, keepdims=True)
            lse = lse_pair[head : head + 1, cols]
            dq = jnp.zeros((HEAD_DIM, BLOCK), F32)
            for source in range(block + 1):
                rows = slice(source * BLOCK, (source + 1) * BLOCK)
                soft = jnp.exp(dot_nt(k_ref[rows, :], queries[head]) - lse)
                if source == block:
                    soft = jnp.where(seen, soft, 0.0)
                dsoft = dot_nt(v_ref[rows, :], grads[head])
                dscore = (soft * (dsoft - delta)).astype(BF16)
                dv = dot_nn(soft.astype(BF16), grads[head])
                dk = dot_nn(dscore, queries[head])
                if head == 0 and source == block:
                    dv_acc[rows, :] = dv
                    dk_acc[rows, :] = dk
                else:
                    dv_acc[rows, :] += dv
                    dk_acc[rows, :] += dk
                dq = dq + dot_nn(k_t[part, rows], dscore)
            dq_t[part, cols] = dq

    lane = lax.broadcasted_iota(jnp.int32, (BLOCK, PAIR), 1)
    for block in range(blocks):
        rows = slice(block * BLOCK, (block + 1) * BLOCK)
        stack_scr[rows, 0:PAIR] = (jnp.transpose(dq_t[:, rows]) * HEAD_DIM**-0.5).astype(BF16)
        stack_scr[rows, PAIR : 2 * PAIR] = dk_acc[rows, :].astype(BF16)
        dv = dv_acc[rows, :]
        stack_scr[rows, 2 * PAIR : 3 * PAIR] = dv.astype(BF16)
        high = dv.astype(BF16)
        low = (dv - high.astype(F32)).astype(BF16)
        fv_acc[rows, :] += dot_nt(high, sel_ref[...]) + dot_nt(low, sel_ref[...])
        one_acc[rows, :] += dot_nt(stack_scr[rows, :], w_scr[...])
    grads_ref[...] = dot_nn(n1_t[...], stack_scr[...])

    @pl.when(step == pl.num_programs(0) - 1)
    def _():
        gain_sum = jnp.zeros((1, width), F32)
        shift_sum = jnp.zeros((1, width), F32)
        for block in range(blocks):
            rows = slice(block * BLOCK, (block + 1) * BLOCK)
            normed, factor = norm_stats(x_ref[rows, :].astype(F32))
            grad_one = one_acc[rows, :]
            gain_sum += jnp.sum(grad_one * normed, axis=0, keepdims=True)
            shift_sum += jnp.sum(grad_one, axis=0, keepdims=True)
            gin_ref[rows, :] = gmix_ref[rows, :] + norm_backward(
                grad_one, normed, factor, gain_ref[...]
            )
            fvg_ref[rows, :] = fv_acc[rows, :]
        vec_ref[...] = jnp.zeros_like(vec_ref)
        vec_ref[0:1, :] = gain_sum
        vec_ref[1:2, :] = shift_sum


def back(scal, tokens, n1, q, k, v, attended, grad_heads, lse, grad_mixed, gain, own, peer, select):
    width = tokens.shape[1]
    own_width = own[0].shape[1]
    half = own_width // PAIR
    fv_width = select.shape[0]
    row_block = pl.BlockSpec((SEQ_LEN, width), lambda i, s: (s[0], 0))
    fixed = lambda shape: pl.BlockSpec(shape, lambda i, s: (0, 0))
    own_block = pl.BlockSpec((width, PAIR), lambda i, s: (0, jnp.minimum(i, half - 1)))
    peer_block = pl.BlockSpec((width, PAIR), lambda i, s: (0, jnp.maximum(i - half, 0)))
    pair_block = pl.BlockSpec((SEQ_LEN, PAIR), lambda i, s: (0, i))
    return pl.pallas_call(
        back_kernel,
        grid_spec=pltpu.PrefetchScalarGridSpec(
            num_scalar_prefetch=1,
            grid=(2 * half,),
            in_specs=[
                row_block,
                fixed((SEQ_LEN, width)),
                pair_block,
                pair_block,
                pair_block,
                pair_block,
                pair_block,
                pl.BlockSpec((1, 2, SEQ_LEN), lambda i, s: (i, 0, 0)),
                fixed((SEQ_LEN, width)),
                fixed((1, width)),
                own_block,
                own_block,
                own_block,
                peer_block,
                peer_block,
                peer_block,
                pl.BlockSpec((fv_width, PAIR), lambda i, s: (0, i)),
            ],
            out_specs=[
                fixed((SEQ_LEN, width)),
                fixed((SEQ_LEN, fv_width)),
                pl.BlockSpec((width, 3 * PAIR), lambda i, s: (0, i)),
                fixed((8, width)),
            ],
            scratch_shapes=[
                pltpu.VMEM((width, SEQ_LEN), BF16),
                pltpu.VMEM((width, 3 * PAIR), BF16),
                pltpu.VMEM((SEQ_LEN, PAIR), F32),
                pltpu.VMEM((SEQ_LEN, PAIR), F32),
                pltpu.VMEM((PAIR, SEQ_LEN), F32),
                pltpu.VMEM((SEQ_LEN, 3 * PAIR), BF16),
                pltpu.VMEM((SEQ_LEN, width), F32),
                pltpu.VMEM((SEQ_LEN, fv_width), F32),
            ],
        ),
        out_shape=[
            jax.ShapeDtypeStruct((SEQ_LEN, width), F32),
            jax.ShapeDtypeStruct((SEQ_LEN, fv_width), F32),
            jax.ShapeDtypeStruct((width, 6 * own_width), F32),
            jax.ShapeDtypeStruct((8, width), F32),
        ],
        compiler_params=pltpu.CompilerParams(vmem_limit_bytes=VMEM_BYTES),
        name="back",
    )(
        scal,
        tokens,
        n1,
        q,
        k,
        v,
        attended,
        grad_heads,
        lse,
        grad_mixed,
        gain,
        *own,
        *peer,
        select,
    )


def swap(value):
    return lax.ppermute(value, "tensor", [(0, 1), (1, 0)])


def on_device(
    tokens,
    first_values,
    seq_count,
    skip_map,
    norm1_gain,
    norm1_shift,
    query_weight,
    key_weight,
    value_weight,
    out_weight,
    norm2_gain,
    norm2_shift,
    up_weight,
    down_weight,
    cotangent,
):
    core = lax.axis_index("tensor")
    width = tokens.shape[1]
    own_width = query_weight.shape[1]
    fresh_width = value_weight.shape[1]
    skip_width = own_width - fresh_width
    fv_width = first_values.shape[1]
    half = own_width // PAIR
    scal = jnp.stack([core, (core < seq_count[0]).astype(jnp.int32)])

    value_padded = jnp.pad(value_weight, ((0, 0), (0, skip_width)))
    own = (query_weight, key_weight, value_padded)
    peer = tuple(swap(w.astype(F32)) for w in own)
    out_peer = swap(out_weight.astype(F32))
    up_peer = swap(up_weight.astype(F32))
    down_peer = swap(down_weight.astype(F32))

    maps = jnp.concatenate([skip_map, swap(skip_map)])
    target = jnp.repeat(maps, HEAD_DIM) * HEAD_DIM + jnp.tile(
        jnp.arange(HEAD_DIM), 2 * skip_width // HEAD_DIM
    )
    target = target.reshape(2, skip_width)
    target = jnp.concatenate([jnp.full((2, fresh_width), -1, jnp.int32), target], axis=1)
    select = (jnp.arange(fv_width)[:, None] == target.reshape(1, 2 * own_width)).astype(BF16)

    gain1, shift1 = norm1_gain[None, :], norm1_shift[None, :]
    gain2, shift2 = norm2_gain[None, :], norm2_shift[None, :]
    n1, q, k, v, attended, lse = front(
        scal, tokens, first_values, gain1, shift1, own, peer, select
    )
    lse = lse[0 : 4 * half].reshape(2 * half, 2, SEQ_LEN)
    (
        layer_rows,
        grad_mixed,
        grad_heads,
        og_own,
        og_peer,
        ug_own,
        dg_own,
        ug_peer,
        dg_peer,
        vec2,
    ) = middle(
        scal,
        tokens,
        attended,
        cotangent,
        gain2,
        shift2,
        out_weight,
        out_peer,
        (up_weight, down_weight),
        (up_peer, down_peer),
    )
    in_rows, fv_rows, proj_grads, vec1 = back(
        scal,
        tokens,
        n1,
        q,
        k,
        v,
        attended,
        grad_heads,
        lse,
        grad_mixed,
        gain1,
        own,
        peer,
        select,
    )
    vectors = jnp.pad(jnp.concatenate([vec1[0:2], vec2[0:2]]).T, ((0, 0), (0, 124)))
    proj_own, proj_peer = proj_grads[:, : 3 * own_width], proj_grads[:, 3 * own_width :]
    packed_own = jnp.concatenate([proj_own, og_own, ug_own, dg_own, vectors], axis=1)
    packed_peer = jnp.concatenate([proj_peer, og_peer, ug_peer, dg_peer, vectors], axis=1)
    packed = packed_own + swap(packed_peer)
    summed = lax.psum_scatter(packed, "dp", scatter_dimension=0, tiled=True)

    proj = summed[:, : 3 * own_width].reshape(-1, half, 3, PAIR)
    query_total = proj[:, :, 0].reshape(-1, own_width)
    key_total = proj[:, :, 1].reshape(-1, own_width)
    value_total = proj[:, :, 2].reshape(-1, own_width)[:, :fresh_width]
    start = 3 * own_width
    out_total = summed[:, start : start + own_width].T
    start += own_width
    ff = up_weight.shape[1]
    up_total = summed[:, start : start + ff]
    down_total = summed[:, start + ff : start + 2 * ff].T
    start += 2 * ff
    gain1_total, shift1_total, gain2_total, shift2_total = (summed[:, start + n] for n in range(4))

    def both(rows):
        other = swap(rows)
        return jnp.where(
            core == 0, jnp.concatenate([rows, other]), jnp.concatenate([other, rows])
        )

    layer_out = both(layer_rows)
    input_grad = both(in_rows)
    side = fv_width // 2
    left, right = fv_rows[:, :side], fv_rows[:, side:]
    keep = jnp.where(core == 0, left, right)
    other = swap(jnp.where(core == 0, right, left))
    first_grad = jnp.where(
        core == 0, jnp.concatenate([keep, other]), jnp.concatenate([other, keep])
    )
    return (
        layer_out,
        input_grad,
        first_grad,
        gain1_total,
        shift1_total,
        query_total,
        key_total,
        value_total,
        out_total,
        gain2_total,
        shift2_total,
        up_total,
        down_total,
    )


def solution(mesh):
    placed = (
        P("dp", None),
        P("dp", None),
        P("dp"),
        P("tensor"),
        P(),
        P(),
        P(None, "tensor"),
        P(None, "tensor"),
        P(None, "tensor"),
        P("tensor", None),
        P(),
        P(),
        P(None, "tensor"),
        P("tensor", None),
        P("dp", None),
    )
    return jax.shard_map(
        on_device,
        mesh=mesh,
        in_specs=placed,
        out_specs=(
            P("dp", None),
            P("dp", None),
            P("dp", "tensor"),
            P("dp"),
            P("dp"),
            P("dp", "tensor"),
            P("dp", "tensor"),
            P("dp", "tensor"),
            P("tensor", "dp"),
            P("dp"),
            P("dp"),
            P("dp", "tensor"),
            P("tensor", "dp"),
        ),
        check_vma=False,
    )
```

time: 835 us -> 489 us (0.59); the launches traced: 820 us -> 483 us
  matrix products: 203 us -> 0 us
  local copies, waits for them, and re-layouts: 231 us -> 45.4 us
  Pallas kernels: 0 us -> 143 us
  other arithmetic: 97.2 us -> 44.9 us
  waiting for transfers between devices: 270 us -> 231 us
    dot_general x48 -> x0, matrix products: 203 us -> none  [the longest x8 37.4 us: causal_scores(): jnp.einsum('qhd,khd->hqk', query_block, seq_keys, preferred_element_type=...]
    pallas_call x0 -> x3, Pallas kernels: none -> 143 us  [the longest x1 55.5 us: middle(): pl.pallas_call(middle_kernel, grid_spec=pltpu.PrefetchScalarGridSpec(num_...]
    dynamic_update_slice x16 -> x0, local copies, waits for them, and re-layouts: 73 us -> none  [the longest x4 58.6 us: attend_backward(): lax.map(one_sequence, (queries, keys_low, values, grad_heads, peaks_all,...]
    psum x3 -> x0, waiting for transfers between devices: 66.8 us -> none  [the longest x1 33.7 us: on_device(): mixed = inputs + lax.psum(attn_part, 'tensor')]
    reduce_sum x12 -> x0, other arithmetic: 43.8 us -> none  [the longest x4 14.5 us: one_block(): row_total = jnp.sum(expo_terms, axis=-1)]
    while x147 -> x0, local copies, waits for them, and re-layouts: 41.2 us -> none
    ppermute x0 -> x11, waiting for transfers between devices: none -> 31.3 us  [swap(): return lax.ppermute(value, 'tensor', [(0, 1), (1, 0)])]
    reshape x12 -> x2, local copies, waits for them, and re-layouts: 32 us -> 1.58 us  [the longest x1 1.49 us: on_device(): lse = lse[0:4 * half].reshape(2 * half, 2, SEQ_LEN)]
  transfers between devices with their start and end apart: 5 -> 12, of which waited for: 5 -> 4; matrix products, arithmetic and copies ran while one was open for 10% -> 8% of each run, Pallas kernels for 0% -> 7%
where the time goes in v2:
time: 489 us; the launch traced here: 483 us
  waiting for transfers between devices  231 us (47%)
  Pallas kernels  143 us (29%)
  local copies, waits for them, and re-layouts  45.4 us (9%)
  other arithmetic  44.9 us (9%)
  between operations  15.4 us (3%)
    reduce_scatter x1, waiting for transfers between devices, on_device(): summed = lax.psum_scatter(packed, 'dp', scatter_dimension=0, tiled=True)  199 us
    pallas_call x1, Pallas kernels, middle(): pl.pallas_call(middle_kernel, grid_spec=pltpu.PrefetchScalarGridSpec(num_...  55.5 us
    pallas_call x1, Pallas kernels, back(): pl.pallas_call(back_kernel, grid_spec=pltpu.PrefetchScalarGridSpec(num_sc...  53 us
    pallas_call x1, Pallas kernels, front(): pl.pallas_call(front_kernel, grid_spec=pltpu.PrefetchScalarGridSpec(num_s...  35 us
    ppermute x11, waiting for transfers between devices, swap(): return lax.ppermute(value, 'tensor', [(0, 1), (1, 0)])  31.3 us
    unnamed x48, local copies, waits for them, and re-layouts  28.3 us
    select_n x2, other arithmetic, both(): jnp.where(core == 0, jnp.concatenate([rows, other]), jnp.concatenate([oth...  15.5 us
    add x1, other arithmetic, on_device(): packed = packed_own + swap(packed_peer)  10.5 us
  transfers between devices with their start and end apart: 12, of which 4 were waited for; matrix products, arithmetic and copies ran while one was open for 8% of the time, Pallas kernels for 7%

profile of v2, /device:TPU:0, one launch (start us, length us, event | category | flops | bytes accessed | tf_op | source)
XLA Modules:
  0.0 483.0 jit_solution(10617122343356850225)
XLA Ops:
  7.2 4.6 convert_element_type.31
  12.3 2.5 convert_element_type.32
  15.0 1.1 copy.36
  17.5 1.1 convert_element_type.26
  19.1 1.1 convert_element_type.27
  20.2 4.7 collective-permute-done.3
  25.3 2.2 convert_element_type.30
  29.6 1.3 broadcast_in_dim.20.gain_ref
  30.9 1.3 broadcast_in_dim.21.shift_ref
  36.3 35.0 %front.1 = (bf16[1024,768]{1,0:T(8,128)(2,1)}, bf16[1024,768]{1,0:T(8,128)(2,1)}, bf16[1024,768]{1,0:T(8,128)(2,1)}, bf16[1024,768]{1,0:T(8,128)(2,1)}, bf16[1024,768]{1,0:T(8,128)(2,1)}, /*index=5*/f32[16,1024]{1,0:T(8,128)}) custom-call(s32[2]{0:T(128)} %pad_add_fusion.scal, bf16[2048,768]{1,0:T(8,128)(2,1)} %x_ref.5, bf16[2048,384]{1,0:T(8,128)(2,1)} %fv_ref.1, ...), custom_call_target="tpu_custom_call" | custom-call | tf_op jit(solution)/shard_map/front/pallas_call | solution.py:164
  71.2 1.5 reshape.45.lse_ref
  72.7 55.5 %middle.1 = (f32[1024,768]{1,0:T(8,128)}, f32[1024,768]{1,0:T(8,128)}, bf16[1024,768]{1,0:T(8,128)(2,1)}, f32[768,384]{1,0:T(8,128)}, f32[768,384]{1,0:T(8,128)}...) custom-call(s32[2]{0:T(128)} %pad_add_fusion.scal, ...), custom_call_target="tpu_custom_call" | custom-call | tf_op jit(solution)/shard_map/middle/pallas_call | solution.py:348
  128.3 53.0 %back.1 = (f32[1024,768]{1,0:T(8,128)}, f32[1024,384]{1,0:T(8,128)}, f32[768,2304]{1,0:T(8,128)}, f32[8,768]{1,0:T(8,128)}) custom-call(s32[2]{0:T(128)} %pad_add_fusion.scal, bf16[2048,768]{1,0:T(8,128)(2,1)} %x_ref.5, bf16[1024,768]{1,0:T(8,128)(2,1)} %get-tuple-element.35.n1_ref, bf16[1024,768]{1,0:T(8,128)(2,1)} %get-tuple-element.36.q_ref, ...), custom_call_target="tpu_custom_call" | custom-call | tf_op jit(solution)/shard_map/back/pallas_call | solution.py:541
  181.3 6.6 %slice_dynamic-update-slice_fusion = (f32[768,4736]{1,0:T(8,128)}, f32[768,4736]{1,0:T(8,128)}) fusion(f32[768,2304]{1,0:T(8,128)} %get-tuple-element.44), kind=kLoop, calls=%fused_computation.2 | loop fusion | bytes 14155776
  189.6 1.1 constant_dynamic-update-slice_fusion.5
  190.8 5.2 %constant_dynamic-update-slice_fusion.4 = f32[768,4736]{1,0:T(8,128)} fusion(f32[768,4736]{1,0:T(8,128)} %constant_dynamic-update-slice_fusion.5, f32[768,1536]{1,0:T(8,128)} %get-tuple-element.51), kind=kLoop, calls=%fused_computation.28 | loop fusion | bytes 9437184
  196.0 1.2 constant_dynamic-update-slice_fusion.2
  197.3 2.7 constant_dynamic-update-slice_fusion.1
  201.0 4.5 constant_dynamic-update-slice_fusion
  206.9 21.8 %collective-permute-done.10 = f32[768,4736]{1,0:T(8,128)S(1)} collective-permute-done((f32[768,4736]{1,0:T(8,128)}, f32[768,4736]{1,0:T(8,128)S(1)}, u32[]{:S(2)}, u32[]{:S(2)}) %collective-permute-start.10) | collective-permute-done | bytes 14549024 | tf_op jit(solution)/shard_map/ppermute | solution.py:609
  228.7 10.5 %add.16 = f32[768,4736]{1,0:T(8,128)} add(f32[768,4736]{1,0:T(8,128)} %get-tuple-element.106, f32[768,4736]{1,0:T(8,128)S(1)} %collective-permute-done.10) | non-fusion elementwise | flops 3637248 | bytes 43646976 | tf_op jit(solution)/shard_map/add | solution.py:702
  239.8 1.9 slice_select_fusion.1
  242.4 4.8 collective-permute-done.9
  247.2 1.3 copy.38
  248.5 2.1 maximum_select_fusion.2
  250.6 1.7 copy.42
  252.3 7.6 %maximum_select_fusion.1 = f32[2048,768]{1,0:T(8,128)} fusion(f32[1024,768]{1,0:T(8,128)} %collective-permute-done.8, f32[1024,768]{1,0:T(8,128)} %get-tuple-element.42, pred[]{:T(512)S(6)} %eq.10), kind=kLoop, calls=%fused_computation.1 | loop fusion | flops 4718592 | bytes 12582913 | tf_op jit(solution)/shard_map/jit(_where)/select_n | solution.py:720
  259.9 7.9 %maximum_select_fusion = f32[2048,768]{1,0:T(8,128)} fusion(f32[1024,768]{1,0:T(8,128)} %collective-permute-done.7, f32[1024,768]{1,0:T(8,128)} %get-tuple-element.34, pred[]{:T(512)S(6)} %eq.10), kind=kLoop, calls=%fused_computation | loop fusion | flops 4718592 | bytes 12582913 | tf_op jit(solution)/shard_map/jit(_where)/select_n | solution.py:720
  267.8 199.2 %reduce-scatter.2.cloned.1.call-done = f32[48,4736]{1,0:T(8,128)} async-done(((f32[768,4736]{1,0:T(8,128)}), f32[48,4736]{1,0:T(8,128)}) %reduce-scatter.2.cloned.1.call-update) | async-done | bytes 909328 | tf_op jit(solution)/shard_map/reduce_scatter | solution.py:703
  470.6 1.9 slice_bitcast_fusion
  472.5 1.5 slice_bitcast_fusion.1
  474.0 1.7 slice_reduce_fusion.3
  (87 shorter events, 17.4 us)
Async XLA Ops:
  7.2 5.2 %copy-start = (bf16[1536,768]{1,0:T(8,128)(2,1)S(1)}, bf16[1536,768]{1,0:T(8,128)(2,1)}, u32[]{:S(2)}) copy-start(bf16[1536,768]{1,0:T(8,128)(2,1)} %down_own.1) | copy-start | bytes 7077892
  7.2 459.8 %reduce-scatter.2.cloned.1.call-start = ((), (), s32[]{:S(2)}) async-start(), calls=%async_computation.1 | async-start | bytes 15458304 | tf_op jit(solution)/shard_map/reduce_scatter | solution.py:703
  11.9 5.6 %copy-start.1 = (bf16[768,384]{1,0:T(8,128)(2,1)S(1)}, bf16[768,384]{1,0:T(8,128)(2,1)}, u32[]{:S(2)}) copy-start(bf16[768,384]{1,0:T(8,128)(2,1)} %wq_own.3) | copy-start | bytes 1769476
  11.9 6.8 %copy-start.10 = (s32[3]{0:T(128)S(1)}, s32[3]{0:T(128)}, u32[]{:S(2)}) copy-start(s32[3]{0:T(128)} %param.18) | copy-start | bytes 40
  11.9 7.2 %copy-start.2 = (bf16[768,384]{1,0:T(8,128)(2,1)S(1)}, bf16[768,384]{1,0:T(8,128)(2,1)}, u32[]{:S(2)}) copy-start(bf16[768,384]{1,0:T(8,128)(2,1)} %wk_own.3) | copy-start | bytes 1769476
  11.9 60.8 %collective-permute-start.5 = (f32[768,1536]{1,0:T(8,128)}, f32[768,1536]{1,0:T(8,128)}, u32[]{:S(2)}, u32[]{:S(2)}) collective-permute-start(f32[768,1536]{1,0:T(8,128)} %convert_element_type.31), channel_id=1, source_target_pairs={{0,1},{1,0},{2,3},{3,2},{4,5},{5,4},{6,7},{7,6},{8,9},{9,8},{10,11... | collective-permute-start | bytes 14155784 | tf_op jit(solution)/shard_map/ppermute | solution.py:609
  14.9 13.5 %copy-start.8 = (f32[768]{0:T(1024)S(1)}, f32[768]{0:T(1024)}, u32[]{:S(2)}) copy-start(f32[768]{0:T(1024)} %param.19) | copy-start | bytes 9220
  14.9 14.1 %copy-start.9 = (f32[768]{0:T(1024)S(1)}, f32[768]{0:T(1024)}, u32[]{:S(2)}) copy-start(f32[768]{0:T(1024)} %param.20) | copy-start | bytes 9220
  14.9 57.8 %collective-permute-start.6 = (f32[1536,768]{1,0:T(8,128)}, f32[1536,768]{1,0:T(8,128)}, u32[]{:S(2)}, u32[]{:S(2)}) collective-permute-start(f32[1536,768]{1,0:T(8,128)} %convert_element_type.32), channel_id=1, source_target_pairs={{0,1},{1,0},{2,3},{3,2},{4,5},{5,4},{6,7},{7,6},{8,9},{9,8},{10,11... | collective-permute-start | bytes 14155784 | tf_op jit(solution)/shard_map/ppermute | solution.py:609
  17.0 10.4 %collective-permute-start.2 = (f32[768,384]{1,0:T(8,128)S(1)}, f32[768,384]{1,0:T(8,128)S(1)}, u32[]{:S(2)}, u32[]{:S(2)}) collective-permute-start(f32[768,384]{1,0:T(8,128)S(1)} %get-tuple-element.107), channel_id=1, source_target_pairs={{0,1},{1,0},{2,3},{3,2},{4,5},{5,4},{6,7},{7,6},{8,9},{9,8},{10,11... | collective-permute-start | bytes 3538952 | tf_op jit(solution)/shard_map/ppermute | solution.py:609
  18.6 16.2 %collective-permute-start = (f32[768,384]{1,0:T(8,128)}, f32[768,384]{1,0:T(8,128)S(1)}, u32[]{:S(2)}, u32[]{:S(2)}) collective-permute-start(f32[768,384]{1,0:T(8,128)} %convert_element_type.26), channel_id=1, source_target_pairs={{0,1},{1,0},{2,3},{3,2},{4,5},{5,4},{6,7},{7,6},{8,9},{9,8},{10,11... | collective-permute-start | bytes 3538952 | tf_op jit(solution)/shard_map/ppermute | solution.py:609
  18.7 6.3 %collective-permute-start.3 = (s32[3]{0:T(128)S(1)}, s32[3]{0:T(128)S(1)}, u32[]{:S(2)}, u32[]{:S(2)}) collective-permute-start(s32[3]{0:T(128)S(1)} %copy-done.10), channel_id=1, source_target_pairs={{0,1},{1,0},{2,3},{3,2},{4,5},{5,4},{6,7},{7,6},{8,9},{9,8},{10,11... | collective-permute-start | bytes 44 | tf_op jit(solution)/shard_map/ppermute | solution.py:609
  24.9 3.4 copy-start.11
  24.9 9.9 %collective-permute-start.1 = (f32[768,384]{1,0:T(8,128)}, f32[768,384]{1,0:T(8,128)S(1)}, u32[]{:S(2)}, u32[]{:S(2)}) collective-permute-start(f32[768,384]{1,0:T(8,128)} %convert_element_type.27), channel_id=1, source_target_pairs={{0,1},{1,0},{2,3},{3,2},{4,5},{5,4},{6,7},{7,6},{8,9},{9,8},{10,11... | collective-permute-start | bytes 3538952 | tf_op jit(solution)/shard_map/ppermute | solution.py:609
  27.5 7.3 %copy-start.3 = (f32[768,384]{1,0:T(8,128)}, f32[768,384]{1,0:T(8,128)S(1)}, u32[]{:S(2)}) copy-start(f32[768,384]{1,0:T(8,128)S(1)} %collective-permute-done.2.wv_peer) | copy-start | bytes 3538948
  27.5 45.2 %collective-permute-start.4 = (f32[384,768]{1,0:T(8,128)}, f32[384,768]{1,0:T(8,128)}, u32[]{:S(2)}, u32[]{:S(2)}) collective-permute-start(f32[384,768]{1,0:T(8,128)} %convert_element_type.30), channel_id=1, source_target_pairs={{0,1},{1,0},{2,3},{3,2},{4,5},{5,4},{6,7},{7,6},{8,9},{9,8},{10,11... | collective-permute-start | bytes 3538952 | tf_op jit(solution)/shard_map/ppermute | solution.py:609
  34.8 1.0 copy-start.4
  34.8 1.4 copy-start.5
  181.3 8.3 %copy-start.7 = (f32[768,384]{1,0:T(8,128)S(1)}, f32[768,384]{1,0:T(8,128)}, u32[]{:S(2)}) copy-start(f32[768,384]{1,0:T(8,128)} %get-tuple-element.50) | copy-start | bytes 3538948
  181.3 18.7 %slice-start.4 = ((s8[4718592]{0:T(1024)(128)(4,1)}), s8[524288]{0:T(1024)(128)(4,1)S(1)}, s32[]{:S(2)}) async-start(s8[4718592]{0:T(1024)(128)(4,1)} %bitcast.27), calls=%async_computation.6 | async-start | bytes 1048576
  189.6 6.4 %copy-start.6 = (f32[768,384]{1,0:T(8,128)S(1)}, f32[768,384]{1,0:T(8,128)}, u32[]{:S(2)}) copy-start(f32[768,384]{1,0:T(8,128)} %get-tuple-element.45) | copy-start | bytes 3538948
  190.8 6.5 %slice-start = ((s8[4718592]{0:T(1024)(128)(4,1)}), s8[4194304]{0:T(1024)(128)(4,1)S(1)}, s32[]{:S(2)}) async-start(s8[4718592]{0:T(1024)(128)(4,1)} %bitcast.23), calls=%async_computation.2 | async-start | bytes 8388608
  190.8 6.5 %slice-start.1 = ((s8[4718592]{0:T(1024)(128)(4,1)}), s8[524288]{0:T(1024)(128)(4,1)S(1)}, s32[]{:S(2)}) async-start(s8[4718592]{0:T(1024)(128)(4,1)} %bitcast.23), calls=%async_computation.3 | async-start | bytes 1048576
  190.8 9.2 %slice-start.5 = ((s8[4718592]{0:T(1024)(128)(4,1)}), s8[4194304]{0:T(1024)(128)(4,1)S(1)}, s32[]{:S(2)}) async-start(s8[4718592]{0:T(1024)(128)(4,1)} %bitcast.27), calls=%async_computation.7 | async-start | bytes 8388608
  196.0 4.6 slice-start.2
  197.3 3.8 slice-start.3
  206.5 22.2 %collective-permute-start.10 = (f32[768,4736]{1,0:T(8,128)}, f32[768,4736]{1,0:T(8,128)S(1)}, u32[]{:S(2)}, u32[]{:S(2)}) collective-permute-start(f32[768,4736]{1,0:T(8,128)} %get-tuple-element.105), channel_id=1, source_target_pairs={{0,1},{1,0},{2,3},{3,2},{4,5},{5,4},{6,7},{7,6},{8,9},{9,8},{10,11... | collective-permute-start | bytes 43646984 | tf_op jit(solution)/shard_map/ppermute | solution.py:609
  239.2 13.1 %collective-permute-start.8 = (f32[1024,768]{1,0:T(8,128)}, f32[1024,768]{1,0:T(8,128)}, u32[]{:S(2)}, u32[]{:S(2)}) collective-permute-start(f32[1024,768]{1,0:T(8,128)} %get-tuple-element.42), channel_id=1, source_target_pairs={{0,1},{1,0},{2,3},{3,2},{4,5},{5,4},{6,7},{7,6},{8,9},{9,8},{10,11... | collective-permute-start | bytes 9437192 | tf_op jit(solution)/shard_map/ppermute | solution.py:609
  239.7 20.2 %collective-permute-start.7 = (f32[1024,768]{1,0:T(8,128)}, f32[1024,768]{1,0:T(8,128)}, u32[]{:S(2)}, u32[]{:S(2)}) collective-permute-start(f32[1024,768]{1,0:T(8,128)} %get-tuple-element.34), channel_id=1, source_target_pairs={{0,1},{1,0},{2,3},{3,2},{4,5},{5,4},{6,7},{7,6},{8,9},{9,8},{10,11... | collective-permute-start | bytes 9437192 | tf_op jit(solution)/shard_map/ppermute | solution.py:609
  242.0 5.2 %collective-permute-start.9 = (f32[1024,192]{0,1:T(8,128)S(1)}, f32[1024,192]{0,1:T(8,128)S(1)}, u32[]{:S(2)}, u32[]{:S(2)}) collective-permute-start(f32[1024,192]{0,1:T(8,128)S(1)} %copy.37), channel_id=1, source_target_pairs={{0,1},{1,0},{2,3},{3,2},{4,5},{5,4},{6,7},{7,6},{8,9},{9,8},{10,11... | collective-permute-start | bytes 2359304 | tf_op jit(solution)/shard_map/ppermute | solution.py:609
Sparse Core Ops, SparseCore 0:
  239.3 227.6 reduce-scatter.1
